TPU v7x, 32 devices: a whole 2x2x4 slice. The times are simulated.
32 devices in a mesh: img: 2 (over x), sub: 16 (over z, y, core).
Axes of the slice: x: 2, y: 2, z: 4, core: 2. Of those that a mesh axis runs over, the one named last changes fastest.
Arguments:
- sub_images: float32 [2, 512, 4096], P(None, ('img', 'sub')), parts along dimension 1, may hold values from -6 to 6
- shift_table: int32 [4, 16, 2, 8], P(None, 'sub'), may hold values from -256 to 256
- phase_table: float32 [4, 16, 2, 8], P(None, 'sub'), may hold values from -3.140625 to 3.140625
- offset_table: int32 [4, 16, 2, 16], P(None, 'sub'), may hold values from 0 to 4
- weight_table: float32 [4, 16, 2, 4, 16], P(None, 'sub'), may hold values from -2 to 2
Outputs:
- turned_image: float32 [2, 8192, 256], P(None, ('img', 'sub')), parts along dimension 1
There are 2 independent parts, one for each index of `img`. A program takes and returns all parts, laid end to end along the dimension named above; an argument that names none is the same for every part. Nothing has to cross between parts.
All inputs are finite; a program needn't handle non-finite values.
Results may differ from a plain program's by a relative error of at most 0.0003.
Values sent between devices are 32-bit elements; how exact they have to be, the bound alone decides.
No kernel may reach another device: no remote copies, remote signals or barrier semaphores. Data moves between devices by JAX's collectives and lax.ppermute only.
A program may use at most 64 MiB of HBM per device.

v0:
```python
import math

import jax
import jax.numpy as jnp
from jax import lax
from jax.sharding import PartitionSpec as P

highest = lax.Precision.HIGHEST


def swapped(block, axis, stride):
    count = lax.axis_size(axis)
    route = []
    for low in range(count):
        high = low | 1 << stride
        if high != low and high < count:
            route += [(low, high), (high, low)]
    return lax.ppermute(block, axis, route)


def fourier_table(length, direction):
    indices = jnp.arange(length, dtype=jnp.int32)
    turns = (indices[:, None] * indices[None, :] % length).astype(jnp.float32)
    angles = turns * (direction * 2.0 * math.pi / length)
    return (jnp.cos(angles), jnp.sin(angles))


def twiddle_table(outer_len, inner_len, direction):
    total = outer_len * inner_len
    outer_idx = jnp.arange(outer_len, dtype=jnp.int32)[:, None]
    inner_idx = jnp.arange(inner_len, dtype=jnp.int32)[None, :]
    turns = (outer_idx * inner_idx % total).astype(jnp.float32)
    angles = turns * (direction * 2.0 * math.pi / total)
    return (jnp.cos(angles), jnp.sin(angles))


def apply_left(table, real_part, imag_part):
    table_real, table_imag = table

    def product(matrix, values):
        return jnp.einsum("kn,bnm->bkm", matrix, values, precision=highest)

    return (
        product(table_real, real_part) - product(table_imag, imag_part),
        product(table_real, imag_part) + product(table_imag, real_part),
    )


def apply_right(table, real_part, imag_part):
    table_real, table_imag = table

    def product(values, matrix):
        return jnp.einsum("bkm,ml->bkl", values, matrix, precision=highest)

    return (
        product(real_part, table_real) - product(imag_part, table_imag),
        product(imag_part, table_real) + product(real_part, table_imag),
    )


def times_table(table, real_part, imag_part):
    table_real, table_imag = table
    return (
        real_part * table_real - imag_part * table_imag,
        real_part * table_imag + imag_part * table_real,
    )


def transform(field, direction):
    outer_len, inner_len = (field.shape[2], field.shape[3])
    left_table = fourier_table(outer_len, direction)
    right_table = fourier_table(inner_len, direction)
    turn_table = twiddle_table(outer_len, inner_len, direction)
    real_part, imag_part = (field[0], field[1])
    if direction < 0:
        real_part, imag_part = apply_left(left_table, real_part, imag_part)
        real_part, imag_part = times_table(turn_table, real_part, imag_part)
        real_part, imag_part = apply_right(right_table, real_part, imag_part)
        return jnp.stack([real_part, imag_part])
    real_part, imag_part = apply_right(right_table, real_part, imag_part)
    real_part, imag_part = times_table(turn_table, real_part, imag_part)
    real_part, imag_part = apply_left(left_table, real_part, imag_part)
    factor = 1.0 / (outer_len * inner_len)
    return jnp.stack([real_part * factor, imag_part * factor])


def rotation(shift_row, phase_row, outer_len, inner_len):
    total = outer_len * inner_len
    outer_idx = jnp.arange(outer_len, dtype=jnp.int32)[:, None]
    inner_idx = jnp.arange(inner_len, dtype=jnp.int32)[None, :]
    flat_idx = outer_idx + outer_len * inner_idx
    signed = (flat_idx + total // 2) % total - total // 2
    turns = (signed[None] * shift_row[:, None, None] % (4 * total)).astype(jnp.float32)
    angles = phase_row[:, None, None] - turns * (2.0 * math.pi / (4 * total))
    return (jnp.cos(angles), jnp.sin(angles))


def rotate(table, field):
    real_part, imag_part = times_table(table, field[0], field[1])
    return jnp.stack([real_part, imag_part])


def blend(matrix, field):
    return jnp.einsum("jm,pmkl->pjkl", matrix, field, precision=highest)


def body(sub_images, shift_table, phase_table, offset_table, weight_table):
    beam_count = sub_images.shape[1]
    half_beams = beam_count // 2
    range_bins = sub_images.shape[2]
    outer_len = 1 << (range_bins.bit_length() - 1) // 2
    inner_len = range_bins // outer_len
    sub_count = lax.axis_size("sub")
    level_count = sub_count.bit_length() - 1
    my_index = lax.axis_index("sub")
    tap_count = weight_table.shape[3]
    columns = jnp.arange(half_beams, dtype=jnp.int32)
    current = sub_images.reshape(2, beam_count, outer_len, inner_len)
    current = transform(current, -1)
    for level_idx in range(level_count):
        side_bit = my_index >> level_idx & 1
        kept_half = lax.dynamic_slice_in_dim(current, side_bit * half_beams, half_beams, 1)
        sent_half = lax.dynamic_slice_in_dim(current, (1 - side_bit) * half_beams, half_beams, 1)
        arrived = swapped(sent_half, "sub", level_idx)
        children = jnp.concatenate([kept_half, arrived], axis=1)
        shift_row = shift_table[level_idx, 0].reshape(2 * half_beams)
        phase_row = phase_table[level_idx, 0].reshape(2 * half_beams)
        turn_factor = rotation(shift_row, phase_row, outer_len, inner_len)
        offsets = offset_table[level_idx, 0]
        weights = weight_table[level_idx, 0]
        stencil = jnp.zeros((2, beam_count, half_beams), jnp.float32)
        for tap_idx in range(tap_count):
            hits = (columns[None, None, :] == offsets[:, :, None] + tap_idx).astype(jnp.float32)
            stencil = stencil + weights[:, tap_idx, :, None] * hits
        matrix = jnp.concatenate([stencil[0], stencil[1]], axis=1)
        current = blend(matrix, rotate(turn_factor, children))
    current = transform(current, 1)
    final_rows = current.reshape(2, beam_count, range_bins)
    turned = jnp.transpose(final_rows, (0, 2, 1))
    return lax.all_to_all(turned, "sub", split_axis=1, concat_axis=2, tiled=True)


def solution(mesh):
    placed = (
        P(None, ("img", "sub"), None),
        P(None, "sub", None, None),
        P(None, "sub", None, None),
        P(None, "sub", None, None),
        P(None, "sub", None, None, None),
    )
    return jax.shard_map(
        body, mesh=mesh, in_specs=placed, out_specs=P(None, ("img", "sub"), None), check_vma=False
    )
```

profile of v0, /device:TPU:0, one launch (start us, length us, event | category | flops | bytes accessed | tf_op | source)
XLA Modules:
  0.0 136.9 jit_solution(9390653000771623887)
XLA Ops:
  0.0 0.1 multiply_sine_fusion.2
  0.1 1.1 fusion.194
  1.2 0.2 squeeze.56
  1.4 0.7 fusion.77
  2.2 0.2 squeeze.57
  2.4 0.7 fusion.75
  3.1 0.7 convolution_subtract_fusion.3
  3.8 0.7 convolution_add_fusion.3
  4.6 0.7 fusion.35
  5.3 0.7 fusion.39
  6.1 0.7 fusion.4
  6.8 0.7 fusion.5
  7.5 0.1 fusion.34
  7.6 0.6 collective-permute-start
  8.4 0.1 mul.803
  8.4 0.1 sub.152
  8.7 1.0 collective-permute-done
  9.7 2.7 %multiply_subtract_fusion.4 = (f32[1,16,64,64]{3,2,1,0:T(8,128)S(1)}, f32[1,16,64,64]{3,2,1,0:T(8,128)S(1)}) fusion(s32[16]{0:T(128)S(1)} %mul.803, s32[64,64]{1,0:T(8,128)S(1)} %fusion.60, f32[16]{0:T(128)S(1)} %sub.152, f32[2,8,64,64]{3,2,1,0:T(8,128)S(1)} %collective-permute-done, f32[2,8,64,64]{3,2,1,0:T(8,128)S(1)} %get-tuple-element.21), kind=kLoop, calls=%fused_computation.108 | loop fusion | flops 1572864 | bytes 1065088 | tf_op jit(solution)/shard_map/sub | solution.py:64
  12.4 0.1 pad_maximum_fusion
  12.6 1.6 %fusion.11 = f32[2,64,64,16]{2,3,1,0:T(8,128)S(1)} fusion(f32[2,16,64,64]{3,2,1,0:T(8,128)S(1)} %pad_maximum_fusion, f32[16,8]{1,0:T(8,128)S(1)} %copy.63, f32[16,8]{1,0:T(8,128)S(1)} %copy.62), kind=kOutput, calls=%fused_computation.36 | convolution fusion | flops 25166080 | bytes 1049600 | tf_op jit(solution)/shard_map/jm,pmkl->pjkl/dot_general | solution.py:104
  14.3 0.1 copy.136
  14.4 3.0 %collective-permute-start.1 = (f32[2,8,64,64]{3,2,1,0:T(8,128)S(1)}, f32[2,8,64,64]{3,2,1,0:T(8,128)S(1)}, u32[]{:S(2)}, u32[]{:S(2)}) collective-permute-start(f32[2,8,64,64]{3,2,1,0:T(8,128)S(1)} %bitcast.190), channel_id=1, source_target_pairs={{0,2},{2,0},{1,3},{3,1},{4,6},{6,4},{5,7},{7,5},{8,10},{10,8},{9,1... | collective-permute-start | bytes 786440 | tf_op jit(solution)/shard_map/ppermute | solution.py:18
  17.3 0.1 mul.825
  17.4 0.1 sub.158
  17.7 0.1 copy.137
  17.8 11.8 %collective-permute-done.1 = f32[2,8,64,64]{3,2,1,0:T(8,128)S(1)} collective-permute-done((f32[2,8,64,64]{3,2,1,0:T(8,128)S(1)}, f32[2,8,64,64]{3,2,1,0:T(8,128)S(1)}, u32[]{:S(2)}, u32[]{:S(2)}) %collective-permute-start.1) | collective-permute-done | bytes 262176 | tf_op jit(solution)/shard_map/ppermute | solution.py:18
  29.6 2.7 %multiply_subtract_fusion.3 = (f32[1,16,64,64]{3,2,1,0:T(8,128)S(1)}, f32[1,16,64,64]{3,2,1,0:T(8,128)S(1)}) fusion(s32[16]{0:T(128)S(1)} %mul.825, s32[64,64]{1,0:T(8,128)S(1)} %fusion.60, f32[16]{0:T(128)S(1)} %sub.158, f32[2,8,64,64]{3,2,1,0:T(8,128)S(1)} %collective-permute-done.1, f32[2,8,64,64]{3,2,1,0:T(8,128)S(1)} %bitcast.187), kind=kLoop, calls=%fused_computation.106 | loop fusion | flops 1572864 | bytes 1065088 | tf_op jit(solution)/shard_map/sub | solution.py:64
  32.3 0.1 pad_maximum_fusion.1
  32.4 1.6 %fusion.9 = f32[2,64,64,16]{2,3,1,0:T(8,128)S(1)} fusion(f32[2,16,64,64]{3,2,1,0:T(8,128)S(1)} %pad_maximum_fusion.1, f32[16,8]{1,0:T(8,128)S(1)} %copy.68, f32[16,8]{1,0:T(8,128)S(1)} %copy.67), kind=kOutput, calls=%fused_computation.34 | convolution fusion | flops 25166080 | bytes 1049600 | tf_op jit(solution)/shard_map/jm,pmkl->pjkl/dot_general | solution.py:104
  34.1 0.1 copy.134
  34.2 1.9 %collective-permute-start.2 = (f32[2,8,64,64]{3,2,1,0:T(8,128)S(1)}, f32[2,8,64,64]{3,2,1,0:T(8,128)S(1)}, u32[]{:S(2)}, u32[]{:S(2)}) collective-permute-start(f32[2,8,64,64]{3,2,1,0:T(8,128)S(1)} %bitcast.189), channel_id=1, source_target_pairs={{0,4},{4,0},{1,5},{5,1},{2,6},{6,2},{3,7},{7,3},{8,12},{12,8},{9,1... | collective-permute-start | bytes 786440 | tf_op jit(solution)/shard_map/ppermute | solution.py:18
  36.6 0.1 copy.135
  36.7 11.0 %collective-permute-done.2 = f32[2,8,64,64]{3,2,1,0:T(8,128)S(1)} collective-permute-done((f32[2,8,64,64]{3,2,1,0:T(8,128)S(1)}, f32[2,8,64,64]{3,2,1,0:T(8,128)S(1)}, u32[]{:S(2)}, u32[]{:S(2)}) %collective-permute-start.2) | collective-permute-done | bytes 262176 | tf_op jit(solution)/shard_map/ppermute | solution.py:18
  47.7 2.7 %multiply_subtract_fusion.2 = (f32[1,16,64,64]{3,2,1,0:T(8,128)S(1)}, f32[1,16,64,64]{3,2,1,0:T(8,128)S(1)}) fusion(s32[16]{0:T(128)S(1)} %mul.847, s32[64,64]{1,0:T(8,128)S(1)} %fusion.60, f32[16]{0:T(128)S(1)} %sub.163, f32[2,8,64,64]{3,2,1,0:T(8,128)S(1)} %collective-permute-done.2, f32[2,8,64,64]{3,2,1,0:T(8,128)S(1)} %bitcast.188), kind=kLoop, calls=%fused_computation.104 | loop fusion | flops 1572864 | bytes 1065088 | tf_op jit(solution)/shard_map/sub | solution.py:64
  50.4 0.1 pad_maximum_fusion.2
  50.5 1.6 %fusion.7 = f32[2,64,64,16]{2,3,1,0:T(8,128)S(1)} fusion(f32[2,16,64,64]{3,2,1,0:T(8,128)S(1)} %pad_maximum_fusion.2, f32[16,8]{1,0:T(8,128)S(1)} %copy.73, f32[16,8]{1,0:T(8,128)S(1)} %copy.72), kind=kOutput, calls=%fused_computation.32 | convolution fusion | flops 25166080 | bytes 1049600 | tf_op jit(solution)/shard_map/jm,pmkl->pjkl/dot_general | solution.py:104
  52.2 0.1 copy.132
  52.3 2.6 %collective-permute-start.3 = (f32[2,8,64,64]{3,2,1,0:T(8,128)S(1)}, f32[2,8,64,64]{3,2,1,0:T(8,128)S(1)}, u32[]{:S(2)}, u32[]{:S(2)}) collective-permute-start(f32[2,8,64,64]{3,2,1,0:T(8,128)S(1)} %bitcast.191), channel_id=1, source_target_pairs={{0,8},{8,0},{1,9},{9,1},{2,10},{10,2},{3,11},{11,3},{4,12},{12,4},... | collective-permute-start | bytes 786440 | tf_op jit(solution)/shard_map/ppermute | solution.py:18
  55.1 0.1 multiply_sine_fusion
  55.2 0.1 copy.133
  55.3 21.7 %collective-permute-done.3 = f32[2,8,64,64]{3,2,1,0:T(8,128)S(1)} collective-permute-done((f32[2,8,64,64]{3,2,1,0:T(8,128)S(1)}, f32[2,8,64,64]{3,2,1,0:T(8,128)S(1)}, u32[]{:S(2)}, u32[]{:S(2)}) %collective-permute-start.3) | collective-permute-done | bytes 262176 | tf_op jit(solution)/shard_map/ppermute | solution.py:18
  77.1 2.9 %multiply_subtract_fusion.1 = (f32[1,16,64,64]{3,2,1,0:T(8,128)S(1)}, f32[1,16,64,64]{3,2,1,0:T(8,128)S(1)}) fusion(s32[16]{0:T(128)S(1)} %mul.869, s32[64,64]{1,0:T(8,128)S(1)} %fusion.60, f32[16]{0:T(128)S(1)} %sub.168, f32[2,8,64,64]{3,2,1,0:T(8,128)S(1)} %collective-permute-done.3, f32[2,8,64,64]{3,2,1,0:T(8,128)S(1)} %bitcast.186), kind=kLoop, calls=%fused_computation.102 | loop fusion | flops 1572864 | bytes 1065088 | tf_op jit(solution)/shard_map/sub | solution.py:64
  80.0 0.1 pad_maximum_fusion.3
  80.1 1.6 %convolution_bitcast_fusion = f32[2,16,64,64]{3,1,2,0:T(8,128)S(1)} fusion(f32[2,16,64,64]{3,2,1,0:T(8,128)S(1)} %pad_maximum_fusion.3, f32[16,8]{1,0:T(8,128)S(1)} %copy.78, f32[16,8]{1,0:T(8,128)S(1)} %copy.77), kind=kOutput, calls=%fused_computation | convolution fusion | flops 25166080 | bytes 1049600 | tf_op jit(solution)/shard_map/jm,pmkl->pjkl/dot_general | solution.py:104
  81.9 0.8 fusion.45
  82.6 0.8 fusion.41
  83.4 0.8 convolution_subtract_fusion.1
  84.2 0.8 convolution_add_fusion.1
  85.0 1.1 fusion.55
  86.1 1.1 fusion.56
  87.2 1.1 fusion.3
  88.3 0.2 copy.86
  88.5 0.2 stack.45
  88.7 1.1 fusion.1
  89.8 0.2 copy.89
  90.0 0.2 stack.46
  90.2 4.4 %copy.90 = f32[2,4096,16]{2,0,1:T(2,128)} copy(f32[2,4096,16]{1,2,0:T(8,128)S(1)} %maximum_bitcast_fusion) | data formatting | bytes 1048576 | tf_op jit(solution)/shard_map/transpose | solution.py:139
  94.6 7.3 %reshape.429 = f32[16,1,8192]{2,1,0:T(1,128)S(1)} reshape(f32[4096,2,16]{2,1,0:T(2,128)} %bitcast.183) | data formatting | bytes 1048576
  101.9 19.5 %all_to_all.18 = f32[16,1,8192]{2,1,0:T(1,128)S(1)} all-to-all(f32[16,1,8192]{2,1,0:T(1,128)S(1)} %reshape.429), channel_id=1, replica_groups=mesh['img'=2,'sub'=16] {'sub'}, dimensions={0} | all-to-all | bytes 1048576 | tf_op jit(solution)/shard_map/all_to_all | solution.py:140
  121.4 0.5 broadcast.938
  121.9 1.9 %reduce = f32[16,8192]{1,0:T(8,128)S(1)} reduce(f32[16,1,8192]{2,1,0:T(1,128)S(1)} %all_to_all.18, f32[]{:T(128)} %broadcast.938), dimensions={1}, to_apply=%all_to_all.13.reduce_sub_computation | reduce | bytes 1048580 | tf_op jit(solution)/shard_map/all_to_all | solution.py:140
  123.8 6.9 %reshape.430 = f32[4096,2,16]{2,1,0:T(2,128)} reshape(f32[16,8192]{1,0:T(8,128)S(1)} %reduce) | data formatting | bytes 1048576
  130.8 5.1 %copy.103 = f32[2,16,256,16]{2,3,1,0:T(8,128)S(1)} copy(f32[2,16,256,16]{3,0,2,1:T(2,128)} %bitcast.184) | data formatting | bytes 1048576 | tf_op jit(solution)/shard_map/all_to_all | solution.py:140
  135.9 1.0 copy.93
  (42 shorter events, 1.4 us)
Async XLA Ops:
  5.3 2.9 %copy-start.1 = (s32[4,1,2,16]{3,2,1,0:T(2,128)S(1)}, s32[4,1,2,16]{3,2,1,0:T(2,128)}, u32[]{:S(2)}) copy-start(s32[4,1,2,16]{3,2,1,0:T(2,128)} %param.8) | copy-start | bytes 1540
  5.3 2.9 %copy-start.2 = (s32[4,1,2,8]{3,2,1,0:T(2,128)S(1)}, s32[4,1,2,8]{3,2,1,0:T(2,128)}, u32[]{:S(2)}) copy-start(s32[4,1,2,8]{3,2,1,0:T(2,128)} %param.6) | copy-start | bytes 772
  5.3 2.9 %copy-start.3 = (f32[4,1,2,8]{3,2,1,0:T(2,128)S(1)}, f32[4,1,2,8]{3,2,1,0:T(2,128)}, u32[]{:S(2)}) copy-start(f32[4,1,2,8]{3,2,1,0:T(2,128)} %param.7) | copy-start | bytes 772
  5.3 2.9 %copy-start = (f32[4,1,2,4,16]{4,3,2,1,0:T(4,128)S(1)}, f32[4,1,2,4,16]{4,3,2,1,0:T(4,128)}, u32[]{:S(2)}) copy-start(f32[4,1,2,4,16]{4,3,2,1,0:T(4,128)} %param.9) | copy-start | bytes 6148
  7.6 2.1 %collective-permute-start = (f32[2,8,64,64]{3,2,1,0:T(8,128)S(1)}, f32[2,8,64,64]{3,2,1,0:T(8,128)S(1)}, u32[]{:S(2)}, u32[]{:S(2)}) collective-permute-start(f32[2,8,64,64]{3,2,1,0:T(8,128)S(1)} %get-tuple-element.22), channel_id=1, source_target_pairs={{0,1},{1,0},{2,3},{3,2},{4,5},{5,4},{6,7},{7,6},{8,9},{9,8},{10,11... | collective-permute-start | bytes 786440 | tf_op jit(solution)/shard_map/ppermute | solution.py:18
  14.4 15.2 %collective-permute-start.1 = (f32[2,8,64,64]{3,2,1,0:T(8,128)S(1)}, f32[2,8,64,64]{3,2,1,0:T(8,128)S(1)}, u32[]{:S(2)}, u32[]{:S(2)}) collective-permute-start(f32[2,8,64,64]{3,2,1,0:T(8,128)S(1)} %bitcast.190), channel_id=1, source_target_pairs={{0,2},{2,0},{1,3},{3,1},{4,6},{6,4},{5,7},{7,5},{8,10},{10,8},{9,1... | collective-permute-start | bytes 786440 | tf_op jit(solution)/shard_map/ppermute | solution.py:18
  34.2 13.5 %collective-permute-start.2 = (f32[2,8,64,64]{3,2,1,0:T(8,128)S(1)}, f32[2,8,64,64]{3,2,1,0:T(8,128)S(1)}, u32[]{:S(2)}, u32[]{:S(2)}) collective-permute-start(f32[2,8,64,64]{3,2,1,0:T(8,128)S(1)} %bitcast.189), channel_id=1, source_target_pairs={{0,4},{4,0},{1,5},{5,1},{2,6},{6,2},{3,7},{7,3},{8,12},{12,8},{9,1... | collective-permute-start | bytes 786440 | tf_op jit(solution)/shard_map/ppermute | solution.py:18
  52.3 24.7 %collective-permute-start.3 = (f32[2,8,64,64]{3,2,1,0:T(8,128)S(1)}, f32[2,8,64,64]{3,2,1,0:T(8,128)S(1)}, u32[]{:S(2)}, u32[]{:S(2)}) collective-permute-start(f32[2,8,64,64]{3,2,1,0:T(8,128)S(1)} %bitcast.191), channel_id=1, source_target_pairs={{0,8},{8,0},{1,9},{9,1},{2,10},{10,2},{3,11},{11,3},{4,12},{12,4},... | collective-permute-start | bytes 786440 | tf_op jit(solution)/shard_map/ppermute | solution.py:18
where the time goes:
time: 137 us
  waiting for transfers between devices  45.6 us (33%)
  local copies, waits for them, and re-layouts  29.7 us (22%)
  matrix products  19.7 us (14%)
  blocking collectives  19.5 us (14%)
  other arithmetic  13.9 us (10%)
  starting transfers between devices  7.95 us (6%)
    ppermute x4, waiting for transfers between devices, swapped(): return lax.ppermute(block, axis, route)  45.6 us
    all_to_all x1, blocking collectives, body(): lax.all_to_all(turned, 'sub', split_axis=1, concat_axis=2, tiled=True)  19.5 us
    unnamed x16, local copies, waits for them, and re-layouts  14.9 us
    sub x4, other arithmetic, times_table(): real_part * table_real - imag_part * table_imag  11.1 us
    ppermute x4, starting transfers between devices, swapped(): return lax.ppermute(block, axis, route)  7.95 us
    dot_general x8, matrix products, product(): return jnp.einsum('kn,bnm->bkm', matrix, values, precision=highest)  7.2 us
    all_to_all x3, local copies, waits for them, and re-layouts, body(): lax.all_to_all(turned, 'sub', split_axis=1, concat_axis=2, tiled=True)  6.64 us
    dot_general x4, matrix products, blend(): return jnp.einsum('jm,pmkl->pjkl', matrix, field, precision=highest)  6.49 us
  transfers between devices with their start and end apart: 4, of which 4 were waited for; matrix products, arithmetic and copies ran while one was open for 1% of the time, Pallas kernels for 0%

commit v1 on v0

v1 whole, which is shorter than its diff:
```python
import functools
import math

import jax
import jax.numpy as jnp
import numpy as np
from jax import lax
from jax.experimental import pallas as pl
from jax.experimental.pallas import tpu as pltpu
from jax.sharding import PartitionSpec as P

LANES = 128
MXU = 256
f32 = jnp.float32
bf16 = jnp.bfloat16


def swapped(block, axis, stride):
    count = lax.axis_size(axis)
    route = []
    for low in range(count):
        high = low | 1 << stride
        if high != low and high < count:
            route += [(low, high), (high, low)]
    return lax.ppermute(block, axis, route)


def whole_spec():
    return pl.BlockSpec(memory_space=pltpu.VMEM)


def call(kernel, outs, ins, scalars, scratch, flops, name):
    moved = sum(math.prod(o.shape) * o.dtype.itemsize for o in outs)
    moved += sum(math.prod(i.shape) * i.dtype.itemsize for i in ins)
    return pl.pallas_call(
        kernel,
        out_shape=outs,
        in_specs=[pl.BlockSpec(memory_space=pltpu.SMEM)] + [whole_spec()] * len(ins),
        out_specs=[whole_spec()] * len(outs),
        scratch_shapes=scratch,
        cost_estimate=pl.CostEstimate(flops=flops, bytes_accessed=moved, transcendentals=0),
        name=name,
    )(scalars, *ins)


def lane_matrix(direction, scale):
    k = np.arange(LANES)
    angle = direction * 2.0 * np.pi * (np.outer(k, k) % LANES) / LANES
    c, s = np.cos(angle) * scale, np.sin(angle) * scale
    full = np.block([[c, s], [-s, c]]).astype(np.float32)
    high = full.astype(bf16)
    low = (full - high.astype(np.float32)).astype(bf16)
    return high, low


def lane_twiddle(outer, direction):
    total = outer * LANES
    turns = np.outer(np.arange(outer), np.arange(LANES)) % total
    angle = direction * 2.0 * np.pi * turns / total
    return np.stack([np.cos(angle), np.sin(angle)]).astype(np.float32)


def times_constant(value, turn):
    real, imag = value
    turn = turn % 1.0
    if turn == 0.0:
        return value
    if turn == 0.5:
        return (-real, -imag)
    if turn == 0.25:
        return (-imag, real)
    if turn == 0.75:
        return (imag, -real)
    c, s = math.cos(2 * math.pi * turn), math.sin(2 * math.pi * turn)
    if abs(abs(c) - abs(s)) < 1e-12:
        r = abs(c)
        sc, ss = math.copysign(1, c), math.copysign(1, s)
        a = (real if sc > 0 else -real) - (imag if ss > 0 else -imag)
        b = (real if ss > 0 else -real) + (imag if sc > 0 else -imag)
        return (a * r, b * r)
    return (real * c - imag * s, real * s + imag * c)


def small_dft(values, direction):
    count = len(values)
    if count == 1:
        return values
    even = small_dft(values[0::2], direction)
    odd = small_dft(values[1::2], direction)
    first, second = [], []
    for k in range(count // 2):
        o = times_constant(odd[k], direction * k / count)
        e = even[k]
        first.append((e[0] + o[0], e[1] + o[1]))
        second.append((e[0] - o[0], e[1] - o[1]))
    return first + second


def split_factors(count):
    inner = 1 << ((count.bit_length() - 1) + 1) // 2
    return count // inner, inner


def staged_dft(count, direction, load, store, scratch):
    outer, inner = split_factors(count)
    for b in range(inner):
        got = small_dft([load(inner * a + b) for a in range(outer)], direction)
        for c in range(outer):
            value = times_constant(got[c], direction * b * c / count)
            scratch[0, c * inner + b] = value[0]
            scratch[1, c * inner + b] = value[1]
    for c in range(outer):
        line = [(scratch[0, c * inner + b], scratch[1, c * inner + b]) for b in range(inner)]
        got = small_dft(line, direction)
        for d in range(inner):
            store(c + outer * d, got[d])


def put_split(high_ref, low_ref, row, rows, value):
    for part in range(2):
        high = value[part].astype(bf16)
        low = (value[part] - high.astype(f32)).astype(bf16)
        high_ref[row : row + rows, part * LANES : (part + 1) * LANES] = high
        low_ref[row : row + rows, part * LANES : (part + 1) * LANES] = low


def dot3(left_high, left_low, right_high, right_low):
    def one(a, b):
        return jnp.dot(a, b, preferred_element_type=f32)

    return one(left_high, right_high) + (one(left_low, right_high) + one(left_high, right_low))


def put_halves(keep_ref, send_ref, bit, k, block, half):
    low, high = block[:half], block[half:]
    keep = jnp.where(bit == 0, low, high)
    send = jnp.where(bit == 0, high, low)
    for part in range(2):
        cut = slice(part * LANES, (part + 1) * LANES)
        keep_ref[part, k] = keep[:, cut]
        send_ref[part, k] = send[:, cut]


def forward_kernel(dims, bits, image, high_m, low_m, twiddle, keep, send, mid, high, low):
    rows, outer, group = dims
    half = rows // 2

    def load(q):
        cut = slice(q * LANES, (q + 1) * LANES)
        return image[0, :, cut], image[1, :, cut]

    def store(k, value):
        c, s = twiddle[0, k : k + 1, :], twiddle[1, k : k + 1, :]
        value = (value[0] * c - value[1] * s, value[0] * s + value[1] * c)
        put_split(high, low, k * rows, rows, value)

    staged_dft(outer, -1, load, store, mid)
    bit = bits[0]
    size = group * rows
    for g in range(outer // group):
        cut = slice(g * size, (g + 1) * size)
        out = dot3(high[cut], low[cut], high_m[...], low_m[...])
        for i in range(group):
            put_halves(keep, send, bit, g * group + i, out[i * rows : (i + 1) * rows], half)


def rotated(value, near, far, k):
    shape = value[0].shape
    fr = jnp.broadcast_to(far[0, :, k : k + 1], shape)
    fi = jnp.broadcast_to(far[1, :, k : k + 1], shape)
    nr, ni = near[0], near[1]
    rr, ri = nr * fr - ni * fi, nr * fi + ni * fr
    return value[0] * rr - value[1] * ri, value[0] * ri + value[1] * rr


def blended(dims, keep, arrived, near, far, blend_high, blend_low, high, low):
    rows, outer, group = dims
    size = group * rows
    for g in range(outer // group):
        for i in range(group):
            k = g * group + i
            value = tuple(
                jnp.concatenate([keep[part, k], arrived[part, k]], axis=0) for part in range(2)
            )
            put_split(high, low, k * rows, rows, rotated(value, near, far, k))
        cut = slice(g * size, (g + 1) * size)
        yield g, dot3(blend_high[...], blend_low[...], high[cut], low[cut])


def level_kernel(dims, level, bits, kept, arrived, near, far, blend_high, blend_low, keep, send, high, low):
    rows, outer, group = dims
    bit = bits[level + 1]
    for g, out in blended(dims, kept, arrived, near, far, blend_high, blend_low, high, low):
        for i in range(group):
            put_halves(keep, send, bit, g * group + i, out[i * rows : (i + 1) * rows], rows // 2)


def inverse_kernel(
    dims, per_block, bits, kept, arrived, near, far, blend_high, blend_low,
    last_near, last_far, high_m, low_m, twiddle, out_ref, mid, back, high, low,
):
    rows, outer, group = dims
    size = group * rows
    for g, out in blended(dims, kept, arrived, near, far, blend_high, blend_low, high, low):
        for i in range(group):
            k = g * group + i
            block = out[i * rows : (i + 1) * rows]
            value = rotated((block[:, :LANES], block[:, LANES:]), last_near, last_far, k)
            put_split(high, low, k * rows, rows, value)
        cut = slice(g * size, (g + 1) * size)
        out = dot3(high[cut], low[cut], high_m[...], low_m[...])
        for i in range(group):
            k = g * group + i
            block = out[i * rows : (i + 1) * rows]
            real, imag = block[:, :LANES], block[:, LANES:]
            c, s = twiddle[0, k : k + 1, :], twiddle[1, k : k + 1, :]
            back[0, k] = real * c - imag * s
            back[1, k] = real * s + imag * c

    def load(k):
        return back[0, k], back[1, k]

    def store(q, value):
        for part in range(2):
            out_ref[q // per_block, part, q % per_block] = value[part]

    staged_dft(outer, 1, load, store, mid)


def turn_kernel(dims, bits, children, blend_high, blend_low, out_ref):
    sub_count, per_block, rows = dims
    beams = sub_count * rows
    for part in range(2):
        for cut in range(per_block):
            line = children[:, part, cut].reshape(beams, LANES).T
            high = line.astype(bf16)
            low = (line - high.astype(f32)).astype(bf16)
            out_ref[part, cut * LANES : (cut + 1) * LANES, :] = dot3(
                high, low, blend_high[...], blend_low[...]
            )


def rotation_tables(shifts, phases, outer):
    full = 4 * outer * LANES
    lane = jnp.arange(LANES, dtype=jnp.int32)
    lane = outer * jnp.where(lane >= LANES // 2, lane - LANES, lane)
    turns = (shifts[..., None] * lane) % full
    angles = phases[..., None] - turns.astype(f32) * (2.0 * math.pi / full)
    near = jnp.stack([jnp.cos(angles), jnp.sin(angles)])
    step = jnp.arange(outer, dtype=jnp.int32)
    angles = ((shifts[..., None] * step) % full).astype(f32) * (2.0 * math.pi / full)
    far = jnp.stack([jnp.cos(angles), -jnp.sin(angles)])
    return near, far


def stencil_of(offsets, weights, half_beams):
    columns = jnp.arange(half_beams, dtype=jnp.int32)
    total = 0.0
    for tap in range(weights.shape[-2]):
        hits = columns == offsets[..., None] + tap
        total = total + jnp.where(hits, weights[..., tap, :, None], 0.0)
    return total


def split(table):
    high = lax.reduce_precision(table, 8, 7)
    return high.astype(bf16), (table - high).astype(bf16)


def body(sub_images, shift_table, phase_table, offset_table, weight_table):
    _, rows, range_bins = sub_images.shape
    half = rows // 2
    outer = range_bins // LANES
    group = max(1, min(outer, MXU // rows))
    sub_count = lax.axis_size("sub")
    levels = sub_count.bit_length() - 1
    last = levels - 1
    me = lax.axis_index("sub")
    taps = weight_table.shape[3]
    dims = (rows, outer, group)
    shifts = shift_table[:, 0]
    phases = phase_table[:, 0]
    offsets = offset_table[:, 0]
    weights = weight_table[:, 0]
    bits = jnp.stack([me >> level & 1 for level in range(levels)]).astype(jnp.int32)

    mine = jnp.concatenate(
        [
            shifts[last].astype(f32).reshape(-1),
            phases[last].reshape(-1),
            offsets[last].astype(f32).reshape(-1),
            weights[last].reshape(-1),
        ]
    )
    width = -(-mine.size // LANES) * LANES
    known = jnp.pad(mine, (0, width - mine.size)).reshape(-1, LANES)
    order = [last] + list(range(last))
    for at in order:
        other = swapped(known, "sub", at)
        if at == last:
            partner = other.reshape(-1)
        mine_first = (me >> at & 1) == 0
        known = jnp.stack([jnp.where(mine_first, known, other), jnp.where(mine_first, other, known)])
    axes = [len(order) - 1 - order.index(at) for at in reversed(range(levels))]
    tables = known.transpose(axes + [levels, levels + 1]).reshape(sub_count, width)
    at = 4 * half
    last_offsets = tables[:, at : at + 2 * rows].astype(jnp.int32).reshape(sub_count, 2, rows)
    at += 2 * rows
    last_weights = tables[:, at : at + 2 * taps * rows].reshape(sub_count, 2, taps, rows)
    last_stencil = stencil_of(last_offsets, last_weights, half)

    partner_shift = partner[half : 2 * half].astype(jnp.int32)
    partner_phase = partner[3 * half : 4 * half]
    own_first = bits[last] == 0
    last_shift = jnp.concatenate(
        [
            jnp.where(own_first, shifts[last, 0], partner_shift),
            jnp.where(own_first, partner_shift, shifts[last, 0]),
        ]
    )
    last_phase = jnp.concatenate(
        [
            jnp.where(own_first, phases[last, 0], partner_phase),
            jnp.where(own_first, partner_phase, phases[last, 0]),
        ]
    )
    near, far = rotation_tables(shifts[:last].reshape(last, rows), phases[:last].reshape(last, rows), outer)
    last_near, last_far = rotation_tables(last_shift, last_phase, outer)

    stencil = stencil_of(offsets[:last], weights[:last], half)
    matrix = jnp.moveaxis(stencil, 1, 2).reshape(last, rows, rows)
    eye = jnp.eye(group, dtype=f32)
    wide = eye[None, :, None, :, None] * matrix[:, None, :, None, :]
    wide_high, wide_low = split(wide.reshape(last, group * rows, group * rows))

    slab = jax.ShapeDtypeStruct((2, outer, half, LANES), f32)
    mid = pltpu.VMEM((2, outer, rows, LANES), f32)
    halves = [pltpu.VMEM((outer * rows, 2 * LANES), bf16)] * 2
    flops = 3 * 2 * outer * rows * MXU * MXU

    keep, send = call(
        functools.partial(forward_kernel, dims),
        [slab, slab],
        [sub_images, *lane_matrix(-1, 1.0), lane_twiddle(outer, -1)],
        bits,
        [mid] + halves,
        flops,
        "forward",
    )
    for level in range(last - 1):
        arrived = swapped(send, "sub", level)
        keep, send = call(
            functools.partial(level_kernel, dims, level),
            [slab, slab],
            [keep, arrived, near[:, level], far[:, level], wide_high[level], wide_low[level]],
            bits,
            halves,
            flops,
            "level",
        )
    level = last - 1
    arrived = swapped(send, "sub", level)
    block = range_bins // sub_count
    direct = block % LANES == 0
    per_block = block // LANES if direct else 1
    (children,) = call(
        functools.partial(inverse_kernel, dims, per_block),
        [jax.ShapeDtypeStruct((outer // per_block, 2, per_block, rows, LANES), f32)],
        [
            keep, arrived, near[:, level], far[:, level], wide_high[level], wide_low[level],
            last_near, last_far, *lane_matrix(1, 1.0 / range_bins), lane_twiddle(outer, 1),
        ],
        bits,
        [mid, mid] + halves,
        2 * flops,
        "inverse",
    )
    index = jnp.arange(sub_count, dtype=jnp.int32)
    if direct and sub_count * rows <= MXU:
        gathered = lax.all_to_all(
            children.reshape(sub_count, 2 * per_block * rows, LANES), "sub", 0, 0, tiled=True
        ).reshape(sub_count, 2, per_block, rows, LANES)
        side = index >> last & 1
        halves_of = jnp.arange(2, dtype=jnp.int32)
        source = index[:, None, None]
        target = index[None, None, :]
        right_half = halves_of[None, :, None] == side[None, None, :]
        own = (source == target) & right_half
        crossed = (source == (target ^ (1 << last))) & right_half
        first = last_stencil[:, 0].transpose(2, 0, 1)
        second = last_stencil[:, 1].transpose(2, 0, 1)
        blend = jnp.where(own[:, :, None, :, None], first[None, None], 0.0)
        blend = blend + jnp.where(crossed[:, :, None, :, None], second[None, None], 0.0)
        blend_high, blend_low = split(blend.reshape(sub_count * rows, sub_count * rows))
        (turned,) = call(
            functools.partial(turn_kernel, (sub_count, per_block, rows)),
            [jax.ShapeDtypeStruct((2, block, sub_count * rows), f32)],
            [gathered, blend_high, blend_low],
            bits,
            [],
            flops,
            "turn",
        )
        return turned
    line = children.reshape(sub_count, outer // sub_count, 2, rows, LANES) if direct else (
        children.reshape(outer, 2, rows, LANES // block, block).transpose(0, 3, 1, 2, 4)
    )
    if direct:
        line = line.transpose(0, 2, 3, 1, 4)
    line = line.reshape(sub_count, 2 * rows, block)
    gathered = lax.all_to_all(line, "sub", 0, 0, tiled=True)
    gathered = gathered.reshape(sub_count, 2, 2, half, block)
    side = (index >> last & 1)[:, None, None, None]
    chosen = jnp.where(side == 0, gathered[:, :, 0], gathered[:, :, 1])
    crossing = gathered[index ^ (1 << last)]
    crossing = jnp.where(side == 0, crossing[:, :, 0], crossing[:, :, 1])
    both = jnp.concatenate([chosen, crossing], axis=2)
    matrix = jnp.moveaxis(last_stencil, 1, 2).reshape(sub_count, rows, rows)
    merged = jnp.einsum("ijm,ipmq->pqij", matrix, both, precision=lax.Precision.HIGHEST)
    return merged.reshape(2, block, sub_count * rows)


def solution(mesh):
    placed = (
        P(None, ("img", "sub"), None),
        P(None, "sub", None, None),
        P(None, "sub", None, None),
        P(None, "sub", None, None),
        P(None, "sub", None, None, None),
    )
    return jax.shard_map(
        body, mesh=mesh, in_specs=placed, out_specs=P(None, ("img", "sub"), None), check_vma=False
    )
```

time: 137 us -> 78 us (0.57)
  waiting for transfers between devices: 45.6 us -> 24.8 us
  matrix products: 19.7 us -> 0 us
  blocking collectives: 19.5 us -> 0 us
  Pallas kernels: 0 us -> 13.4 us
  local copies, waits for them, and re-layouts: 29.7 us -> 17.9 us
  other arithmetic: 13.9 us -> 7.75 us
  starting transfers between devices: 7.95 us -> 13.4 us
    ppermute x4 -> x7, waiting for transfers between devices: 45.6 us -> 12.7 us  [swapped(): return lax.ppermute(block, axis, route)]
    dot_general x20 -> x0, matrix products: 19.7 us -> none  [the longest x8 7.2 us: product(): return jnp.einsum('kn,bnm->bkm', matrix, values, precision=highest)]
    all_to_all x1 -> x0, blocking collectives: 19.5 us -> none  [body(): lax.all_to_all(turned, 'sub', split_axis=1, concat_axis=2, tiled=True)]
    pallas_call x0 -> x5, Pallas kernels: none -> 13.4 us  [call(): pl.pallas_call(kernel, out_shape=outs, in_specs=[pl.BlockSpec(memory_spac...]
    all_to_all x0 -> x1, waiting for transfers between devices: none -> 12.1 us  [body(): lax.all_to_all(children.reshape(sub_count, 2 * per_block * rows, LANES),...]
    unnamed x16 -> x13, local copies, waits for them, and re-layouts: 14.9 us -> 2.9 us
    sub x5 -> x0, other arithmetic: 11.1 us -> none  [the longest x4 11.1 us: times_table(): real_part * table_real - imag_part * table_imag]
    mul x6 -> x5, local copies, waits for them, and re-layouts: 0.72 us -> 9.42 us  [the longest x4 9.34 us: body(): wide = eye[None, :, None, :, None] * matrix[:, None, :, None, :]]
  transfers between devices with their start and end apart: 4 -> 8, of which waited for: 4 -> 4; matrix products, arithmetic and copies ran while one was open for 1% -> 25% of each run, Pallas kernels for 0% -> 7%
where the time goes in v1:
time: 78 us; the launch traced here: 77.4 us
  waiting for transfers between devices  24.8 us (32%)
  local copies, waits for them, and re-layouts  17.9 us (23%)
  starting transfers between devices  13.4 us (17%)
  Pallas kernels  13.4 us (17%)
  other arithmetic  7.75 us (10%)
    pallas_call x5, Pallas kernels, call(): pl.pallas_call(kernel, out_shape=outs, in_specs=[pl.BlockSpec(memory_spac...  13.4 us
    ppermute x7, waiting for transfers between devices, swapped(): return lax.ppermute(block, axis, route)  12.7 us
    all_to_all x1, waiting for transfers between devices, body(): lax.all_to_all(children.reshape(sub_count, 2 * per_block * rows, LANES),...  12.1 us
    ppermute x7, starting transfers between devices, swapped(): return lax.ppermute(block, axis, route)  9.8 us
    mul x4, local copies, waits for them, and re-layouts, body(): wide = eye[None, :, None, :, None] * matrix[:, None, :, None, :]  9.34 us
    all_to_all x1, starting transfers between devices, body(): lax.all_to_all(children.reshape(sub_count, 2 * per_block * rows, LANES),...  3.57 us
    unnamed x13, local copies, waits for them, and re-layouts  2.9 us
  transfers between devices with their start and end apart: 8, of which 4 were waited for; matrix products, arithmetic and copies ran while one was open for 25% of the time, Pallas kernels for 7%

profile of v1, /device:TPU:0, one launch (start us, length us, event | category | flops | bytes accessed | tf_op | source)
XLA Modules:
  0.0 77.4 jit_solution(14891841978327562826)
XLA Ops:
  0.0 0.7 slice.145
  0.7 0.1 reshape_squeeze.7
  0.8 0.7 slice_convert_fusion.2
  1.5 0.1 convert_element_type.103
  1.5 0.7 slice_convert_fusion.1
  2.2 0.1 convert_element_type.105
  2.3 0.7 slice.143
  3.0 0.1 reshape_squeeze.6
  3.1 0.1 fusion.45
  3.2 4.1 %collective-permute-start.3 = (f32[2,128]{1,0:T(2,128)S(1)}, f32[2,128]{1,0:T(2,128)S(1)}, u32[]{:S(2)}, u32[]{:S(2)}) collective-permute-start(f32[2,128]{1,0:T(2,128)S(1)} %fusion.45), channel_id=1, source_target_pairs={{0,8},{8,0},{1,9},{9,1},{2,10},{10,2},{3,11},{11,3},{4,12},{12,4},... | collective-permute-start | bytes 3080 | tf_op jit(solution)/shard_map/ppermute | solution.py:25
  7.2 0.6 pad_add_fusion.bits
  7.9 2.5 %forward.1 = (f32[2,32,8,128]{3,2,1,0:T(8,128)}, f32[2,32,8,128]{3,2,1,0:T(8,128)}) custom-call(s32[4]{0:T(128)} %pad_add_fusion.bits, f32[2,16,4096]{2,1,0:T(8,128)} %image.1, bf16[256,256]{1,0:T(8,128)(2,1)} %constant.87.clone.high_m, bf16[256,256]{1,0:T(8,128)(2,1)} %constant.88.clone.low_m, f32[2,32,128]{2,1,0:T(8,128)} %constant.89.clone.twiddle), custom_call_target="tpu_custom_call" | custom-call | flops 201326592 | bytes 1343488 | tf_op jit(solution)/shard_map/forward/pallas_call | solution.py:35
  10.4 0.7 slice_bitcast_fusion.8
  11.1 0.7 fusion.42
  11.8 0.7 slice_bitcast_fusion.9
  12.5 0.1 eq.246
  12.6 0.1 fusion.9
  12.7 0.1 copy.20
  12.8 3.3 %mul.215 = f32[3,16,16,16,16]{4,3,2,1,0:T(8,128)} broadcast(f32[3,16,16]{2,1,0:T(8,128)S(1)} %copy.20), dimensions={0,2,4} | broadcast | bytes 789504 | tf_op jit(solution)/shard_map/mul | solution.py:333
  16.1 4.9 %mul.216 = f32[3,256,256]{2,1,0:T(8,128)S(1)} reshape(f32[3,16,16,16,16]{4,3,2,1,0:T(8,128)} %mul.215) | data formatting | bytes 1572864 | tf_op jit(solution)/shard_map/mul | solution.py:333
  21.0 0.2 mul.212
  21.2 0.9 %mul.213 = f32[256,256]{1,0:T(8,128)S(1)} reshape(f32[16,16,16,16]{3,2,1,0:T(8,128)S(1)} %mul.212) | data formatting | bytes 524288 | tf_op jit(solution)/shard_map/mul | solution.py:333
  22.2 0.1 mul.200
  22.3 0.1 sub.52
  22.4 0.2 sine_negate_fusion
  22.5 0.1 fusion
  22.7 0.9 %slice_bitcast_fusion = (bf16[256,256]{1,0:T(8,128)(2,1)}, bf16[256,256]{1,0:T(8,128)(2,1)}, bf16[256,256]{1,0:T(8,128)(2,1)}, bf16[256,256]{1,0:T(8,128)(2,1)},...) fusion(bf16[3,256,256]{2,1,0:T(8,128)(2,1)S(1)} %get-tuple-element.17, bf16[3,256,256]{2,1,0:T(8,128)(2,1)S(1)} %get-tuple-element.18), kind=kLoop, calls=%fused_computation.7 | loop fusion | bytes 1572864 | tf_op jit(solution)/shard_map/squeeze | solution.py:370
  23.6 0.2 fusion.26
  23.8 0.6 fusion.24
  24.4 0.6 fusion.23
  25.1 0.1 select_bitcast_fusion.7
  25.2 0.5 collective-permute-start.4
  25.7 0.1 broadcast_select_fusion.1
  25.8 0.1 broadcast_select_fusion.3
  25.9 0.1 pad_add_fusion.1
  25.9 0.1 fusion.38
  26.1 0.1 pad_maximum_fusion.8
  26.1 0.1 fusion.40
  26.3 0.6 pad_maximum_fusion.2.last_near
  26.9 1.6 %collective-permute-start.5 = (f32[2,2,2,128]{3,2,0,1:T(2,128)S(1)}, f32[2,2,2,128]{3,2,0,1:T(2,128)S(1)}, u32[]{:S(2)}, u32[]{:S(2)}) collective-permute-start(f32[2,2,2,128]{3,2,0,1:T(2,128)S(1)} %pad_maximum_fusion.6), channel_id=1, source_target_pairs={{0,2},{2,0},{1,3},{3,1},{4,6},{6,4},{5,7},{7,5},{8,10},{10,8},{9,1... | collective-permute-start | bytes 12296 | tf_op jit(solution)/shard_map/ppermute | solution.py:25
  28.5 0.6 pad_maximum_fusion.3.last_far
  29.1 1.5 %collective-permute-done.5 = f32[2,2,2,128]{3,2,0,1:T(2,128)S(1)} collective-permute-done((f32[2,2,2,128]{3,2,0,1:T(2,128)S(1)}, f32[2,2,2,128]{3,2,0,1:T(2,128)S(1)}, u32[]{:S(2)}, u32[]{:S(2)}) %collective-permute-start.5) | collective-permute-done | bytes 4128 | tf_op jit(solution)/shard_map/ppermute | solution.py:25
  30.6 1.6 %collective-permute-start.6 = (f32[2,2,2,2,128]{4,3,1,0,2:T(2,128)S(1)}, f32[2,2,2,2,128]{4,3,1,0,2:T(2,128)S(1)}, u32[]{:S(2)}, u32[]{:S(2)}) collective-permute-start(f32[2,2,2,2,128]{4,3,1,0,2:T(2,128)S(1)} %pad_maximum_fusion.5), channel_id=1, source_target_pairs={{0,4},{4,0},{1,5},{5,1},{2,6},{6,2},{3,7},{7,3},{8,12},{12,8},{9,1... | collective-permute-start | bytes 24584 | tf_op jit(solution)/shard_map/ppermute | solution.py:25
  32.2 0.7 copy-done.1
  32.9 2.6 %level.2 = (f32[2,32,8,128]{3,2,1,0:T(8,128)}, f32[2,32,8,128]{3,2,1,0:T(8,128)}) custom-call(s32[4]{0:T(128)} %pad_add_fusion.bits, f32[2,32,8,128]{3,2,1,0:T(8,128)} %get-tuple-element.11.kept, f32[2,32,8,128]{3,2,1,0:T(8,128)} %copy-done.1, f32[2,16,128]{2,1,0:T(8,128)} %get-tuple-element.37.near, f32[2,16,32]{2,1,0:T(8,128)} %get-tuple-element.34.far, ...), custom_call_target="tpu_custom_call" | custom-call | flops 201326592 | bytes 1331200 | tf_op jit(solution)/shard_map/level/pallas_call | solution.py:35
  35.5 1.5 %collective-permute-start.1 = (f32[2,32,8,128]{3,2,1,0:T(8,128)}, f32[2,32,8,128]{3,2,1,0:T(8,128)S(1)}, u32[]{:S(2)}, u32[]{:S(2)}) collective-permute-start(f32[2,32,8,128]{3,2,1,0:T(8,128)} %get-tuple-element.14), channel_id=1, source_target_pairs={{0,2},{2,0},{1,3},{3,1},{4,6},{6,4},{5,7},{7,5},{8,10},{10,8},{9,1... | collective-permute-start | bytes 786440 | tf_op jit(solution)/shard_map/ppermute | solution.py:25
  37.1 5.4 %collective-permute-done.1.arrived = f32[2,32,8,128]{3,2,1,0:T(8,128)S(1)} collective-permute-done((f32[2,32,8,128]{3,2,1,0:T(8,128)}, f32[2,32,8,128]{3,2,1,0:T(8,128)S(1)}, u32[]{:S(2)}, u32[]{:S(2)}) %collective-permute-start.1) | collective-permute-done | bytes 262176 | tf_op jit(solution)/shard_map/ppermute | solution.py:25
  42.6 0.7 copy-done.3
  43.3 2.6 %level.3 = (f32[2,32,8,128]{3,2,1,0:T(8,128)}, f32[2,32,8,128]{3,2,1,0:T(8,128)}) custom-call(s32[4]{0:T(128)} %pad_add_fusion.bits, f32[2,32,8,128]{3,2,1,0:T(8,128)} %get-tuple-element.13.kept, f32[2,32,8,128]{3,2,1,0:T(8,128)} %copy-done.3, f32[2,16,128]{2,1,0:T(8,128)} %get-tuple-element.38.near, f32[2,16,32]{2,1,0:T(8,128)} %get-tuple-element.35.far, ...), custom_call_target="tpu_custom_call" | custom-call | flops 201326592 | bytes 1331200 | tf_op jit(solution)/shard_map/level/pallas_call | solution.py:35
  45.9 0.4 collective-permute-start.2
  46.3 0.1 slice_convert_fusion
  46.4 0.1 slice.178
  46.5 0.1 reshape.634
  46.6 0.1 eq.273
  46.7 5.7 %collective-permute-done.2.arrived = f32[2,32,8,128]{3,2,1,0:T(8,128)S(1)} collective-permute-done((f32[2,32,8,128]{3,2,1,0:T(8,128)}, f32[2,32,8,128]{3,2,1,0:T(8,128)S(1)}, u32[]{:S(2)}, u32[]{:S(2)}) %collective-permute-start.2) | collective-permute-done | bytes 262176 | tf_op jit(solution)/shard_map/ppermute | solution.py:25
  52.5 0.7 copy-done.2
  53.2 3.3 %inverse.1 = f32[16,2,2,16,128]{4,3,2,1,0:T(8,128)} custom-call(s32[4]{0:T(128)} %pad_add_fusion.bits, f32[2,32,8,128]{3,2,1,0:T(8,128)} %get-tuple-element.15.kept, f32[2,32,8,128]{3,2,1,0:T(8,128)} %copy-done.2, f32[2,16,128]{2,1,0:T(8,128)} %get-tuple-element.36.near, f32[2,16,32]{2,1,0:T(8,128)} %get-tuple-element.33.far, ...), custom_call_target="tpu_custom_call" | custom-call | flops 402653184 | bytes 1646592 | tf_op jit(solution)/shard_map/inverse/pallas_call | solution.py:35
  56.4 3.6 %all-to-all-start = ((f32[16,64,128]{2,1,0:T(8,128)}), f32[16,64,128]{2,1,0:T(8,128)S(1)}, u32[]{:S(2)}, u32[]{:S(2)}) async-start(f32[16,64,128]{2,1,0:T(8,128)} %bitcast.165), calls=%async_computation | async-start | bytes 1048576 | tf_op jit(solution)/shard_map/all_to_all | solution.py:380
  60.2 0.3 select_add_fusion
  60.5 0.9 %add.208 = f32[256,256]{1,0:T(8,128)S(1)} reshape(f32[16,2,8,16,16]{4,3,2,1,0:T(8,128)S(1)} %select_add_fusion) | data formatting | bytes 524288 | tf_op jit(solution)/shard_map/add | solution.py:393
  61.5 0.7 fusion.1
  62.2 12.1 %all-to-all-done = f32[16,64,128]{2,1,0:T(8,128)S(1)} async-done(((f32[16,64,128]{2,1,0:T(8,128)}), f32[16,64,128]{2,1,0:T(8,128)S(1)}, u32[]{:S(2)}, u32[]{:S(2)}) %all-to-all-start) | async-done | bytes 524320 | tf_op jit(solution)/shard_map/all_to_all | solution.py:380
  74.3 0.8 %copy-done = f32[16,64,128]{2,1,0:T(8,128)} copy-done((f32[16,64,128]{2,1,0:T(8,128)}, f32[16,64,128]{2,1,0:T(8,128)S(1)}, u32[]{:S(2)}) %copy-start) | copy-done | bytes 524312
  75.0 2.4 %turn.1 = f32[2,256,256]{2,1,0:T(8,128)} custom-call(s32[4]{0:T(128)} %pad_add_fusion.bits, f32[16,2,2,16,128]{4,3,2,1,0:T(8,128)} %bitcast.164, bf16[256,256]{1,0:T(8,128)(2,1)} %get-tuple-element.26.blend_high, bf16[256,256]{1,0:T(8,128)(2,1)} %get-tuple-element.25.blend_low), custom_call_target="tpu_custom_call" | custom-call | flops 201326592 | bytes 1310720 | tf_op jit(solution)/shard_map/turn/pallas_call | solution.py:35
  (46 shorter events, 0.3 us)
Async XLA Ops:
  3.2 21.9 %collective-permute-start.3 = (f32[2,128]{1,0:T(2,128)S(1)}, f32[2,128]{1,0:T(2,128)S(1)}, u32[]{:S(2)}, u32[]{:S(2)}) collective-permute-start(f32[2,128]{1,0:T(2,128)S(1)} %fusion.45), channel_id=1, source_target_pairs={{0,8},{8,0},{1,9},{9,1},{2,10},{10,2},{3,11},{11,3},{4,12},{12,4},... | collective-permute-start | bytes 3080 | tf_op jit(solution)/shard_map/ppermute | solution.py:25
  10.4 21.9 %collective-permute-start = (f32[2,32,8,128]{3,2,1,0:T(8,128)}, f32[2,32,8,128]{3,2,1,0:T(8,128)S(1)}, u32[]{:S(2)}, u32[]{:S(2)}) collective-permute-start(f32[2,32,8,128]{3,2,1,0:T(8,128)} %get-tuple-element.12), channel_id=1, source_target_pairs={{0,1},{1,0},{2,3},{3,2},{4,5},{5,4},{6,7},{7,6},{8,9},{9,8},{10,11... | collective-permute-start | bytes 786440 | tf_op jit(solution)/shard_map/ppermute | solution.py:25
  21.0 1.2 %slice-start = ((s32[4,1,2,8]{3,2,1,0:T(2,128)}), s32[3,1,2,8]{3,2,1,0:T(2,128)S(1)}, s32[]{:S(2)}) async-start(s32[4,1,2,8]{3,2,1,0:T(2,128)} %param.12), calls=%async_computation.1 | async-start | bytes 6144 | tf_op jit(solution)/shard_map/slice | solution.py:327
  21.0 1.3 %slice-start.1 = ((f32[4,1,2,8]{3,2,1,0:T(2,128)}), f32[3,1,2,8]{3,2,1,0:T(2,128)S(1)}, s32[]{:S(2)}) async-start(f32[4,1,2,8]{3,2,1,0:T(2,128)} %param.13), calls=%async_computation.2 | async-start | bytes 6144 | tf_op jit(solution)/shard_map/slice | solution.py:327
  22.2 3.5 %copy-start.4 = (s32[4,1,2,8]{3,2,1,0:T(2,128)S(1)}, s32[4,1,2,8]{3,2,1,0:T(2,128)}, u32[]{:S(2)}) copy-start(s32[4,1,2,8]{3,2,1,0:T(2,128)} %param.12) | copy-start | bytes 772
  22.2 3.6 %copy-start.5 = (f32[4,1,2,8]{3,2,1,0:T(2,128)S(1)}, f32[4,1,2,8]{3,2,1,0:T(2,128)}, u32[]{:S(2)}) copy-start(f32[4,1,2,8]{3,2,1,0:T(2,128)} %param.13) | copy-start | bytes 772
  25.2 1.7 %collective-permute-start.4 = (f32[2,2,128]{2,1,0:T(2,128)S(1)}, f32[2,2,128]{2,1,0:T(2,128)S(1)}, u32[]{:S(2)}, u32[]{:S(2)}) collective-permute-start(f32[2,2,128]{2,1,0:T(2,128)S(1)} %pad_maximum_fusion.7), channel_id=1, source_target_pairs={{0,1},{1,0},{2,3},{3,2},{4,5},{5,4},{6,7},{7,6},{8,9},{9,8},{10,11... | collective-permute-start | bytes 6152 | tf_op jit(solution)/shard_map/ppermute | solution.py:25
  26.9 3.7 %collective-permute-start.5 = (f32[2,2,2,128]{3,2,0,1:T(2,128)S(1)}, f32[2,2,2,128]{3,2,0,1:T(2,128)S(1)}, u32[]{:S(2)}, u32[]{:S(2)}) collective-permute-start(f32[2,2,2,128]{3,2,0,1:T(2,128)S(1)} %pad_maximum_fusion.6), channel_id=1, source_target_pairs={{0,2},{2,0},{1,3},{3,1},{4,6},{6,4},{5,7},{7,5},{8,10},{10,8},{9,1... | collective-permute-start | bytes 12296 | tf_op jit(solution)/shard_map/ppermute | solution.py:25
  30.6 6.5 %collective-permute-start.6 = (f32[2,2,2,2,128]{4,3,1,0,2:T(2,128)S(1)}, f32[2,2,2,2,128]{4,3,1,0,2:T(2,128)S(1)}, u32[]{:S(2)}, u32[]{:S(2)}) collective-permute-start(f32[2,2,2,2,128]{4,3,1,0,2:T(2,128)S(1)} %pad_maximum_fusion.5), channel_id=1, source_target_pairs={{0,4},{4,0},{1,5},{5,1},{2,6},{6,2},{3,7},{7,3},{8,12},{12,8},{9,1... | collective-permute-start | bytes 24584 | tf_op jit(solution)/shard_map/ppermute | solution.py:25
  32.2 0.7 copy-start.1
  35.5 7.0 %collective-permute-start.1 = (f32[2,32,8,128]{3,2,1,0:T(8,128)}, f32[2,32,8,128]{3,2,1,0:T(8,128)S(1)}, u32[]{:S(2)}, u32[]{:S(2)}) collective-permute-start(f32[2,32,8,128]{3,2,1,0:T(8,128)} %get-tuple-element.14), channel_id=1, source_target_pairs={{0,2},{2,0},{1,3},{3,1},{4,6},{6,4},{5,7},{7,5},{8,10},{10,8},{9,1... | collective-permute-start | bytes 786440 | tf_op jit(solution)/shard_map/ppermute | solution.py:25
  42.6 0.7 copy-start.3
  45.9 6.6 %collective-permute-start.2 = (f32[2,32,8,128]{3,2,1,0:T(8,128)}, f32[2,32,8,128]{3,2,1,0:T(8,128)S(1)}, u32[]{:S(2)}, u32[]{:S(2)}) collective-permute-start(f32[2,32,8,128]{3,2,1,0:T(8,128)} %get-tuple-element.16), channel_id=1, source_target_pairs={{0,4},{4,0},{1,5},{5,1},{2,6},{6,2},{3,7},{7,3},{8,12},{12,8},{9,1... | collective-permute-start | bytes 786440 | tf_op jit(solution)/shard_map/ppermute | solution.py:25
  52.5 0.7 copy-start.2
  56.4 17.8 %all-to-all-start = ((f32[16,64,128]{2,1,0:T(8,128)}), f32[16,64,128]{2,1,0:T(8,128)S(1)}, u32[]{:S(2)}, u32[]{:S(2)}) async-start(f32[16,64,128]{2,1,0:T(8,128)} %bitcast.165), calls=%async_computation | async-start | bytes 1048576 | tf_op jit(solution)/shard_map/all_to_all | solution.py:380
  74.3 0.8 %copy-start = (f32[16,64,128]{2,1,0:T(8,128)}, f32[16,64,128]{2,1,0:T(8,128)S(1)}, u32[]{:S(2)}) copy-start(f32[16,64,128]{2,1,0:T(8,128)S(1)} %all-to-all-done) | copy-start | bytes 1572868

commit v2 on v1

v2 whole, which is shorter than its diff:
```python
import functools
import math

import jax
import jax.numpy as jnp
import numpy as np
from jax import lax
from jax.experimental import pallas as pl
from jax.experimental.pallas import tpu as pltpu
from jax.sharding import PartitionSpec as P

LANES = 128
MXU = 256
VMEM_GRANT = 12 << 20
f32 = jnp.float32
bf16 = jnp.bfloat16


def swapped(block, axis, stride):
    count = lax.axis_size(axis)
    route = []
    for low in range(count):
        high = low | 1 << stride
        if high != low and high < count:
            route += [(low, high), (high, low)]
    return lax.ppermute(block, axis, route)


def call(kernel, outs, ins, scratch, flops, name):
    moved = sum(math.prod(o.shape) * o.dtype.itemsize for o in outs)
    moved += sum(math.prod(i.shape) * i.dtype.itemsize for i in ins)
    return pl.pallas_call(
        kernel,
        out_shape=outs,
        in_specs=[pl.BlockSpec(memory_space=pltpu.VMEM)] * len(ins),
        out_specs=[pl.BlockSpec(memory_space=pltpu.VMEM)] * len(outs),
        scratch_shapes=scratch,
        cost_estimate=pl.CostEstimate(flops=flops, bytes_accessed=moved, transcendentals=0),
        compiler_params=pltpu.CompilerParams(vmem_limit_bytes=VMEM_GRANT),
        name=name,
    )(*ins)


def lane_matrix(direction, scale):
    k = np.arange(LANES)
    angle = direction * 2.0 * np.pi * (np.outer(k, k) % LANES) / LANES
    c, s = np.cos(angle) * scale, np.sin(angle) * scale
    full = np.block([[c, s], [-s, c]]).astype(np.float32)
    high = full.astype(bf16)
    low = (full - high.astype(np.float32)).astype(bf16)
    return high, low


def lane_twiddle(outer, direction):
    total = outer * LANES
    turns = np.outer(np.arange(outer), np.arange(LANES)) % total
    angle = direction * 2.0 * np.pi * turns / total
    return np.stack([np.cos(angle), np.sin(angle)]).astype(np.float32)


def times_constant(value, turn):
    real, imag = value
    turn = turn % 1.0
    if turn == 0.0:
        return value
    if turn == 0.5:
        return (-real, -imag)
    if turn == 0.25:
        return (-imag, real)
    if turn == 0.75:
        return (imag, -real)
    c, s = math.cos(2 * math.pi * turn), math.sin(2 * math.pi * turn)
    if abs(abs(c) - abs(s)) < 1e-12:
        r = abs(c)
        sc, ss = math.copysign(1, c), math.copysign(1, s)
        a = (real if sc > 0 else -real) - (imag if ss > 0 else -imag)
        b = (real if ss > 0 else -real) + (imag if sc > 0 else -imag)
        return (a * r, b * r)
    return (real * c - imag * s, real * s + imag * c)


def small_dft(values, direction):
    count = len(values)
    if count == 1:
        return values
    even = small_dft(values[0::2], direction)
    odd = small_dft(values[1::2], direction)
    first, second = [], []
    for k in range(count // 2):
        o = times_constant(odd[k], direction * k / count)
        e = even[k]
        first.append((e[0] + o[0], e[1] + o[1]))
        second.append((e[0] - o[0], e[1] - o[1]))
    return first + second


def split_factors(count):
    inner = 1 << ((count.bit_length() - 1) + 1) // 2
    return count // inner, inner


def staged_dft(count, direction, load, store, scratch):
    outer, inner = split_factors(count)
    for b in range(inner):
        got = small_dft([load(inner * a + b) for a in range(outer)], direction)
        for c in range(outer):
            value = times_constant(got[c], direction * b * c / count)
            scratch[0, c * inner + b] = value[0]
            scratch[1, c * inner + b] = value[1]
    for c in range(outer):
        line = [(scratch[0, c * inner + b], scratch[1, c * inner + b]) for b in range(inner)]
        got = small_dft(line, direction)
        for d in range(inner):
            store(c + outer * d, got[d])


def put_split(high_ref, low_ref, row, rows, value):
    for part in range(2):
        high = value[part].astype(bf16)
        low = (value[part] - high.astype(f32)).astype(bf16)
        high_ref[row : row + rows, part * LANES : (part + 1) * LANES] = high
        low_ref[row : row + rows, part * LANES : (part + 1) * LANES] = low


def dot3(left_high, left_low, right_high, right_low):
    def one(a, b):
        return jnp.dot(a, b, preferred_element_type=f32)

    return one(left_high, right_high) + (one(left_low, right_high) + one(left_high, right_low))


def put_halves(keep_ref, send_ref, bit, outer, k, block, half):
    low, high = block[:half], block[half:]
    keep = jnp.where(bit == 0, low, high)
    send = jnp.where(bit == 0, high, low)
    for part in range(2):
        cut = slice(part * LANES, (part + 1) * LANES)
        keep_ref[part * outer + k] = keep[:, cut]
        send_ref[part * outer + k] = send[:, cut]


def cos_sin(turns, full):
    quarter = full // 4
    turns = turns & (full - 1)
    quadrant = (turns + quarter // 2) >> (quarter.bit_length() - 1)
    x = (turns - quadrant * quarter).astype(f32) * (2.0 * math.pi / full)
    y = x * x
    sine, cosine = 0.0, 0.0
    for term in (9, 7, 5, 3, 1):
        sine = sine * y + (-1.0) ** (term // 2) / math.factorial(term)
    for term in (10, 8, 6, 4, 2, 0):
        cosine = cosine * y + (-1.0) ** (term // 2) / math.factorial(term)
    sine = sine * x
    odd = (quadrant & 1) == 1
    first = jnp.where(odd, sine, cosine)
    second = jnp.where(odd, cosine, sine)
    first = jnp.where(((quadrant + 1) & 2) == 2, -first, first)
    return first, jnp.where((quadrant & 2) == 2, -second, second)


class Sizes:
    def __init__(self, rows, outer, taps, sub_count):
        self.rows, self.outer, self.taps, self.sub_count = rows, outer, taps, sub_count
        self.half = rows // 2
        self.levels = sub_count.bit_length() - 1
        self.last = self.levels - 1
        self.group = max(1, min(outer, MXU // rows))
        self.at_offset = 2 * taps
        self.at_shift = self.at_offset + 2
        self.at_phase = self.at_shift + 2
        self.record = -(-(self.at_phase + 2) // 8) * 8
        self.pages = -(-self.levels * self.record // LANES)
        self.slots = LANES // rows
        self.blocks = -(-sub_count // self.slots)
        self.known = self.blocks * self.record // 8
        self.last_page = self.last * self.record // LANES


def prep_kernel(z, shift, phase, offset, weight, tabs, pack, lines):
    me = lax.axis_index("sub")
    lines[...] = jnp.zeros_like(lines)
    for level in range(z.levels):
        at = level * z.record
        for c in range(2):
            lines[at + c * z.taps : at + (c + 1) * z.taps, : z.rows] = weight[level, 0, c]
        at += z.at_offset
        lines[at : at + 2, : z.rows] = offset[level, 0].astype(f32)
        lines[at + 2 : at + 4, : z.half] = shift[level, 0].astype(f32)
        lines[at + 4 : at + 6, : z.half] = phase[level, 0]
    for page in range(z.pages):
        turned = lines[page * LANES : (page + 1) * LANES, :].T[: z.rows]
        tabs[:, page * LANES : (page + 1) * LANES] = turned
        if page == z.last_page:
            pack[: z.rows] = turned
    spread = lines[z.last * z.record : (z.last + 1) * z.record, :]
    step = z.rows
    while step < LANES:
        spread = spread + pltpu.roll(spread, step, 1)
        step *= 2
    slot = lax.broadcasted_iota(jnp.int32, spread.shape, 1) // z.rows
    for block in range(z.blocks):
        at = z.rows + block * z.record
        pack[at : at + z.record] = jnp.where(slot + block * z.slots == me, spread, 0.0)


def tables_kernel(z, tabs, pack, other, near, far, wide_high, wide_low):
    me = lax.axis_index("sub")
    full = 4 * z.outer * LANES
    shape = (z.rows, LANES)
    lane = lax.broadcasted_iota(jnp.int32, shape, 1)
    signed = z.outer * jnp.where(lane >= LANES // 2, lane - LANES, lane)

    def children(table, at):
        return [table[: z.half, at + c : at + c + 1] for c in range(2)]

    for level in range(z.levels):
        at = level * z.record
        shifts, phases = children(tabs, at + z.at_shift), children(tabs, at + z.at_phase)
        if level == z.last:
            away = at - z.last_page * LANES
            theirs = children(other, away + z.at_shift)[1], children(other, away + z.at_phase)[1]
            low = (me >> level & 1) == 0
            for mine, their in zip((shifts, phases), theirs):
                first = mine[0]
                mine[0] = jnp.where(low, first, their)
                mine[1] = jnp.where(low, their, first)
        shifts = jnp.broadcast_to(jnp.concatenate(shifts, axis=0), shape).astype(jnp.int32)
        phases = jnp.broadcast_to(jnp.concatenate(phases, axis=0), shape)
        c, s = cos_sin(shifts * signed, full)
        pc, ps = jnp.cos(phases), jnp.sin(phases)
        near[level, 0] = pc * c + ps * s
        near[level, 1] = ps * c - pc * s
        c, s = cos_sin(shifts * lane, full)
        far[level, 0] = c
        far[level, 1] = -s

    size = z.group * z.rows
    shape = (z.rows, size)
    column = lax.broadcasted_iota(jnp.int32, shape, 1)
    beam = column % z.half
    child = (column // z.half) % 2
    block = column // z.rows
    for level in range(z.last):
        at = level * z.record
        wide = jnp.zeros(shape, f32)
        for c in range(2):
            first = tabs[:, at + z.at_offset + c : at + z.at_offset + c + 1].astype(jnp.int32)
            for tap in range(z.taps):
                hits = (beam == first + tap) & (child == c)
                wide += jnp.where(hits, tabs[:, at + c * z.taps + tap : at + c * z.taps + tap + 1], 0.0)
        for i in range(z.group):
            value = jnp.where(block == i, wide, 0.0)
            high = value.astype(bf16)
            wide_high[level, i * z.rows : (i + 1) * z.rows] = high
            wide_low[level, i * z.rows : (i + 1) * z.rows] = (value - high.astype(f32)).astype(bf16)


def last_blend_kernel(z, known, blend_high, blend_low):
    beams = z.sub_count * z.rows
    for block in range(beams // LANES):
        table = known[block * z.record : (block + 1) * z.record]
        shape = (z.rows, LANES)
        row = lax.broadcasted_iota(jnp.int32, shape, 0)
        owner = lax.broadcasted_iota(jnp.int32, shape, 1) // z.rows + block * z.slots
        mine = (row // z.half) == (owner >> z.last & 1)
        parts = []
        for c in range(2):
            first = jnp.broadcast_to(table[z.at_offset + c : z.at_offset + c + 1].astype(jnp.int32), shape)
            total = jnp.zeros(shape, f32)
            for tap in range(z.taps):
                hits = (row % z.half == first + tap) & mine
                line = jnp.broadcast_to(table[c * z.taps + tap : c * z.taps + tap + 1], shape)
                total += jnp.where(hits, line, 0.0)
            parts.append(total)
        for source in range(z.sub_count):
            value = jnp.where(owner == source, parts[0], 0.0)
            value = jnp.where(owner == source ^ (1 << z.last), parts[1], value)
            high = value.astype(bf16)
            at = (slice(source * z.rows, (source + 1) * z.rows), slice(block * LANES, (block + 1) * LANES))
            blend_high[at] = high
            blend_low[at] = (value - high.astype(f32)).astype(bf16)


def forward_kernel(z, image, high_m, low_m, twiddle, keep, send, mid, high, low):
    def load(q):
        cut = slice(q * LANES, (q + 1) * LANES)
        return image[0, :, cut], image[1, :, cut]

    def store(k, value):
        c, s = twiddle[0, k : k + 1, :], twiddle[1, k : k + 1, :]
        value = (value[0] * c - value[1] * s, value[0] * s + value[1] * c)
        put_split(high, low, k * z.rows, z.rows, value)

    staged_dft(z.outer, -1, load, store, mid)
    bit = lax.axis_index("sub") & 1
    size = z.group * z.rows
    for g in range(z.outer // z.group):
        cut = slice(g * size, (g + 1) * size)
        out = dot3(high[cut], low[cut], high_m[...], low_m[...])
        for i in range(z.group):
            block = out[i * z.rows : (i + 1) * z.rows]
            put_halves(keep, send, bit, z.outer, g * z.group + i, block, z.half)


def rotated(value, near, far, k):
    shape = value[0].shape
    fr = jnp.broadcast_to(far[0][:, k : k + 1], shape)
    fi = jnp.broadcast_to(far[1][:, k : k + 1], shape)
    nr, ni = near[0], near[1]
    rr, ri = nr * fr - ni * fi, nr * fi + ni * fr
    return value[0] * rr - value[1] * ri, value[0] * ri + value[1] * rr


def blended(z, level, keep, arrived, near, far, wide_high, wide_low, high, low):
    size = z.group * z.rows
    close = near[level, 0], near[level, 1]
    steps = far[level, 0], far[level, 1]
    for g in range(z.outer // z.group):
        for i in range(z.group):
            k = g * z.group + i
            value = tuple(
                jnp.concatenate([keep[part * z.outer + k], arrived[part * z.outer + k]], axis=0)
                for part in range(2)
            )
            put_split(high, low, k * z.rows, z.rows, rotated(value, close, steps, k))
        cut = slice(g * size, (g + 1) * size)
        yield g, dot3(wide_high[level], wide_low[level], high[cut], low[cut])


def level_kernel(z, level, kept, arrived, held, near, far, wide_high, wide_low, keep, send, high, low):
    slabs = 2 * z.outer
    bit = lax.axis_index("sub") >> (level + 1) & 1
    if level == 0:
        send[slabs:] = held[...]
    else:
        send[slabs:] = held[slabs:] + arrived[slabs:]
    for g, out in blended(z, level, kept, arrived, near, far, wide_high, wide_low, high, low):
        for i in range(z.group):
            block = out[i * z.rows : (i + 1) * z.rows]
            put_halves(keep, send, bit, z.outer, g * z.group + i, block, z.half)


def inverse_kernel(
    z, per_block, kept, arrived, held, near, far, wide_high, wide_low, high_m, low_m, twiddle,
    out_ref, known, mid, back, high, low,
):
    slabs = 2 * z.outer
    size = z.group * z.rows
    level = z.last - 1
    known[...] = held[slabs:] + arrived[slabs:] if level > 0 else held[...]
    close = near[z.last, 0], near[z.last, 1]
    steps = far[z.last, 0], far[z.last, 1]
    for g, out in blended(z, level, kept, arrived, near, far, wide_high, wide_low, high, low):
        for i in range(z.group):
            k = g * z.group + i
            block = out[i * z.rows : (i + 1) * z.rows]
            value = rotated((block[:, :LANES], block[:, LANES:]), close, steps, k)
            put_split(high, low, k * z.rows, z.rows, value)
        cut = slice(g * size, (g + 1) * size)
        out = dot3(high[cut], low[cut], high_m[...], low_m[...])
        for i in range(z.group):
            k = g * z.group + i
            block = out[i * z.rows : (i + 1) * z.rows]
            real, imag = block[:, :LANES], block[:, LANES:]
            c, s = twiddle[0, k : k + 1, :], twiddle[1, k : k + 1, :]
            back[0, k] = real * c - imag * s
            back[1, k] = real * s + imag * c

    def load(k):
        return back[0, k], back[1, k]

    def store(q, value):
        for part in range(2):
            out_ref[q // per_block, part, q % per_block] = value[part]

    staged_dft(z.outer, 1, load, store, mid)


def turn_kernel(z, per_block, children, blend_high, blend_low, out_ref):
    beams = z.sub_count * z.rows
    for part in range(2):
        for cut in range(per_block):
            line = children[:, part, cut].reshape(beams, LANES).T
            high = line.astype(bf16)
            low = (line - high.astype(f32)).astype(bf16)
            out_ref[part, cut * LANES : (cut + 1) * LANES, :] = dot3(
                high, low, blend_high[...], blend_low[...]
            )


def body(sub_images, shift_table, phase_table, offset_table, weight_table):
    _, rows, range_bins = sub_images.shape
    outer = range_bins // LANES
    sub_count = lax.axis_size("sub")
    z = Sizes(rows, outer, weight_table.shape[3], sub_count)
    size = z.group * rows
    flops = 3 * 2 * outer * rows * MXU * MXU
    shape = jax.ShapeDtypeStruct

    tabs, pack = call(
        functools.partial(prep_kernel, z),
        [shape((rows, z.pages * LANES), f32), shape((rows + z.blocks * z.record, LANES), f32)],
        [shift_table, phase_table, offset_table, weight_table],
        [pltpu.VMEM((z.pages * LANES, LANES), f32)],
        1 << 16,
        "prep",
    )
    other = swapped(pack, "sub", z.last)

    slabs = 2 * outer
    slab = shape((slabs, z.half, LANES), f32)
    longer = shape((slabs + z.known, z.half, LANES), f32)
    mid = pltpu.VMEM((2, outer, rows, LANES), f32)
    halves = [pltpu.VMEM((outer * rows, 2 * LANES), bf16)] * 2

    keep, send = call(
        functools.partial(forward_kernel, z),
        [slab, slab],
        [sub_images, *lane_matrix(-1, 1.0), lane_twiddle(outer, -1)],
        [mid] + halves,
        flops,
        "forward",
    )
    held = pack[rows:] + other[rows:]
    arrived = swapped(send, "sub", 0)
    held = (held + swapped(held, "sub", 0)).reshape(z.known, 8, LANES)
    tables = call(
        functools.partial(tables_kernel, z),
        [shape((z.levels, 2, rows, LANES), f32)] * 2 + [shape((z.last, size, size), bf16)] * 2,
        [tabs, pack, other],
        [],
        1 << 20,
        "tables",
    )
    for level in range(z.last - 1):
        keep, send = call(
            functools.partial(level_kernel, z, level),
            [slab, longer],
            [keep, arrived, held, *tables],
            halves,
            flops,
            "level",
        )
        held = send
        arrived = swapped(send, "sub", level + 1)
    block = range_bins // sub_count
    direct = block % LANES == 0
    per_block = block // LANES if direct else 1
    children, known = call(
        functools.partial(inverse_kernel, z, per_block),
        [
            shape((outer // per_block, 2, per_block, rows, LANES), f32),
            shape((z.known, 8, LANES), f32),
        ],
        [keep, arrived, held, *tables, *lane_matrix(1, 1.0 / range_bins), lane_twiddle(outer, 1)],
        [mid, mid] + halves,
        2 * flops,
        "inverse",
    )
    known = known.reshape(z.blocks * z.record, LANES)
    beams = sub_count * rows
    if direct and beams <= MXU:
        gathered = lax.all_to_all(
            children.reshape(sub_count, 2 * per_block * rows, LANES), "sub", 0, 0, tiled=True
        ).reshape(sub_count, 2, per_block, rows, LANES)
        blend = call(
            functools.partial(last_blend_kernel, z),
            [shape((beams, beams), bf16)] * 2,
            [known],
            [],
            1 << 18,
            "blend",
        )
        (turned,) = call(
            functools.partial(turn_kernel, z, per_block),
            [shape((2, block, beams), f32)],
            [gathered, *blend],
            [],
            flops,
            "turn",
        )
        return turned
    return wide_turn(z, block, direct, children, known)


def wide_turn(z, block, direct, children, known):
    sub_count, rows, half = z.sub_count, z.rows, z.half
    if direct:
        line = children.transpose(0, 1, 3, 2, 4)
    else:
        line = children.reshape(z.outer, 2, rows, LANES // block, block).transpose(0, 3, 1, 2, 4)
    gathered = lax.all_to_all(line.reshape(sub_count, 2 * rows, block), "sub", 0, 0, tiled=True)
    gathered = gathered.reshape(sub_count, 2, 2, half, block)
    table = known.reshape(z.blocks, z.record, z.slots, rows).transpose(0, 2, 1, 3)
    table = table.reshape(-1, z.record, rows)[:sub_count]
    weights = table[:, : z.at_offset].reshape(sub_count, 2, z.taps, rows)
    offsets = table[:, z.at_offset : z.at_shift].astype(jnp.int32)
    columns = jnp.arange(half, dtype=jnp.int32)
    stencil = 0.0
    for tap in range(z.taps):
        hits = columns == offsets[..., None] + tap
        stencil = stencil + jnp.where(hits, weights[:, :, tap, :, None], 0.0)
    index = jnp.arange(sub_count, dtype=jnp.int32)
    side = (index >> z.last & 1)[:, None, None, None]
    chosen = jnp.where(side == 0, gathered[:, :, 0], gathered[:, :, 1])
    crossing = gathered[index ^ (1 << z.last)]
    crossing = jnp.where(side == 0, crossing[:, :, 0], crossing[:, :, 1])
    both = jnp.concatenate([chosen, crossing], axis=2)
    matrix = jnp.moveaxis(stencil, 1, 2).reshape(sub_count, rows, rows)
    merged = jnp.einsum("ijm,ipmq->pqij", matrix, both, precision=lax.Precision.HIGHEST)
    return merged.reshape(2, block, sub_count * rows)


def solution(mesh):
    placed = (
        P(None, ("img", "sub"), None),
        P(None, "sub", None, None),
        P(None, "sub", None, None),
        P(None, "sub", None, None),
        P(None, "sub", None, None, None),
    )
    return jax.shard_map(
        body, mesh=mesh, in_specs=placed, out_specs=P(None, ("img", "sub"), None), check_vma=False
    )
```

time: 78 us -> 52.6 us (0.67)
  local copies, waits for them, and re-layouts: 17.9 us -> 5.65 us
  other arithmetic: 7.75 us -> 0.01 us
  Pallas kernels: 13.4 us -> 5.83 us
  waiting for transfers between devices: 24.8 us -> 28.3 us
  starting transfers between devices: 13.4 us -> 12.2 us
    mul x5 -> x0, local copies, waits for them, and re-layouts: 9.42 us -> none  [the longest x4 9.34 us: body(): wide = eye[None, :, None, :, None] * matrix[:, None, :, None, :]]
    pallas_call x5 -> x8, Pallas kernels: 13.4 us -> 5.83 us  [call(): pl.pallas_call(kernel, out_shape=outs, in_specs=[pl.BlockSpec(memory_spac...]
    unnamed x13 -> x22, local copies, waits for them, and re-layouts: 2.9 us -> 5.65 us
    convert_element_type x6 -> x0, other arithmetic: 2.31 us -> none  [the longest x2 0.87 us: split(): return (high.astype(bf16), (table - high).astype(bf16))]
    slice x10 -> x0, local copies, waits for them, and re-layouts: 2.22 us -> none  [the longest x1 0.71 us: body(): stencil = stencil_of(offsets[:last], weights[:last], half)]
    all_to_all x1, waiting for transfers between devices: 12.1 us -> 14.2 us  [body(): lax.all_to_all(children.reshape(sub_count, 2 * per_block * rows, LANES),...]
    another operation x11 -> x0, other arithmetic: 1.98 us -> none  [the longest x1 0.65 us: body(): jnp.stack([me >> level & 1 for level in range(levels)]).astype(jnp.int32)]
    ppermute x7 -> x5, starting transfers between devices: 9.8 us -> 7.97 us  [swapped(): return lax.ppermute(block, axis, route)]
  transfers between devices with their start and end apart: 8 -> 6, of which waited for: 4 -> 4; matrix products, arithmetic and copies ran while one was open for 25% -> 0% of each run, Pallas kernels for 7% -> 2%
where the time goes in v2:
time: 52.6 us; the launch traced here: 52.1 us
  waiting for transfers between devices  28.3 us (54%)
  starting transfers between devices  12.2 us (23%)
  Pallas kernels  5.83 us (11%)
  local copies, waits for them, and re-layouts  5.65 us (11%)
    all_to_all x1, waiting for transfers between devices, body(): lax.all_to_all(children.reshape(sub_count, 2 * per_block * rows, LANES),...  14.2 us
    ppermute x5, waiting for transfers between devices, swapped(): return lax.ppermute(block, axis, route)  14.1 us
    ppermute x5, starting transfers between devices, swapped(): return lax.ppermute(block, axis, route)  7.97 us
    pallas_call x8, Pallas kernels, call(): pl.pallas_call(kernel, out_shape=outs, in_specs=[pl.BlockSpec(memory_spac...  5.83 us
    unnamed x22, local copies, waits for them, and re-layouts  5.65 us
    all_to_all x1, starting transfers between devices, body(): lax.all_to_all(children.reshape(sub_count, 2 * per_block * rows, LANES),...  4.28 us
  transfers between devices with their start and end apart: 6, of which 4 were waited for; matrix products, arithmetic and copies ran while one was open for 0% of the time, Pallas kernels for 2%

profile of v2, /device:TPU:0, one launch (start us, length us, event | category | flops | bytes accessed | tf_op | source)
XLA Modules:
  0.0 52.1 jit_solution(12343653398869581880)
XLA Ops:
  0.0 0.0 copy-start.6
  0.0 0.0 copy-start.7
  0.0 0.7 %copy-done.7 = f32[4,1,2,4,16]{4,3,2,1,0:T(4,128)S(1)} copy-done((f32[4,1,2,4,16]{4,3,2,1,0:T(4,128)S(1)}, f32[4,1,2,4,16]{4,3,2,1,0:T(4,128)}, u32[]{:S(2)}) %copy-start.7) | copy-done | bytes 2072
  0.7 0.0 copy-start.8
  0.7 0.7 %copy-done.8 = s32[4,1,2,8]{3,2,1,0:T(2,128)S(1)} copy-done((s32[4,1,2,8]{3,2,1,0:T(2,128)S(1)}, s32[4,1,2,8]{3,2,1,0:T(2,128)}, u32[]{:S(2)}) %copy-start.8) | copy-done | bytes 280
  1.4 0.0 copy-start.9
  1.4 0.7 %copy-done.9 = f32[4,1,2,8]{3,2,1,0:T(2,128)S(1)} copy-done((f32[4,1,2,8]{3,2,1,0:T(2,128)S(1)}, f32[4,1,2,8]{3,2,1,0:T(2,128)}, u32[]{:S(2)}) %copy-start.9) | copy-done | bytes 280
  2.1 0.0 copy-start.10
  2.1 0.7 %copy-done.10 = s32[4,1,2,16]{3,2,1,0:T(2,128)S(1)} copy-done((s32[4,1,2,16]{3,2,1,0:T(2,128)S(1)}, s32[4,1,2,16]{3,2,1,0:T(2,128)}, u32[]{:S(2)}) %copy-start.10) | copy-done | bytes 536
  2.8 0.2 prep.1
  3.0 4.1 %collective-permute-start.1 = (f32[48,128]{1,0:T(8,128)S(1)}, f32[48,128]{1,0:T(8,128)S(1)}, u32[]{:S(2)}, u32[]{:S(2)}) collective-permute-start(f32[48,128]{1,0:T(8,128)S(1)} %get-tuple-element.23.pack), channel_id=1, source_target_pairs={{0,8},{8,0},{1,9},{9,1},{2,10},{10,2},{3,11},{11,3},{4,12},{12,4},... | collective-permute-start | bytes 73736 | tf_op jit(solution)/shard_map/ppermute | solution.py:26
  7.1 0.0 copy-done.6
  7.1 0.0 copy-start
  7.1 1.0 %copy-done = f32[2,16,4096]{2,1,0:T(8,128)S(1)} copy-done((f32[2,16,4096]{2,1,0:T(8,128)S(1)}, f32[2,16,4096]{2,1,0:T(8,128)}, u32[]{:S(2)}) %copy-start) | copy-done | bytes 524312
  8.2 0.0 copy-start.3
  8.2 0.9 %copy-done.3 = bf16[256,256]{1,0:T(8,128)(2,1)S(1)} copy-done((bf16[256,256]{1,0:T(8,128)(2,1)S(1)}, bf16[256,256]{1,0:T(8,128)(2,1)}, u32[]{:S(2)}) %copy-start.3) | copy-done | bytes 131096
  9.1 0.0 copy-start.4
  9.1 0.9 %copy-done.4 = bf16[256,256]{1,0:T(8,128)(2,1)S(1)} copy-done((bf16[256,256]{1,0:T(8,128)(2,1)S(1)}, bf16[256,256]{1,0:T(8,128)(2,1)}, u32[]{:S(2)}) %copy-start.4) | copy-done | bytes 131096
  10.0 0.6 %forward.1 = (f32[64,8,128]{2,1,0:T(8,128)S(1)}, f32[64,8,128]{2,1,0:T(8,128)S(1)}) custom-call(f32[2,16,4096]{2,1,0:T(8,128)S(1)} %copy-done, bf16[256,256]{1,0:T(8,128)(2,1)S(1)} %copy-done.4, bf16[256,256]{1,0:T(8,128)(2,1)S(1)} %copy-done.3, f32[2,32,128]{2,1,0:T(8,128)S(1)} %copy-done.6), custom_call_target="tpu_custom_call" | custom-call | flops 201326592 | bytes 1343488 | tf_op jit(solution)/shard_map/forward/pallas_call | solution.py:32
  10.5 0.1 collective-permute-start
  10.6 0.0 collective-permute-done.1.other
  10.6 0.5 %collective-permute-start.2 = (f32[32,128]{1,0:T(8,128)S(1)}, f32[32,128]{1,0:T(8,128)S(1)}, u32[]{:S(2)}, u32[]{:S(2)}) collective-permute-start(f32[32,128]{1,0:T(8,128)S(1)} %slice_add_fusion), channel_id=1, source_target_pairs={{0,1},{1,0},{2,3},{3,2},{4,5},{5,4},{6,7},{7,6},{8,9},{9,8},{10,11... | collective-permute-start | bytes 49160 | tf_op jit(solution)/shard_map/ppermute | solution.py:26
  11.2 0.5 tables.1
  11.6 0.5 collective-permute-done.2
  12.2 0.0 collective-permute-done.arrived
  12.2 0.7 %level.2 = (f32[64,8,128]{2,1,0:T(8,128)S(1)}, f32[68,8,128]{2,1,0:T(8,128)S(1)}) custom-call(f32[64,8,128]{2,1,0:T(8,128)S(1)} %get-tuple-element.21.kept, f32[64,8,128]{2,1,0:T(8,128)S(1)} %collective-permute-done.arrived, f32[4,8,128]{2,1,0:T(8,128)S(1)} %add_bitcast_fusion.held, f32[4,2,16,128]{3,2,1,0:T(8,128)S(1)} %get-tuple-element.25.near, ...), custom_call_target="tpu_custom_call" | custom-call | flops 201326592 | bytes 1998848 | tf_op jit(solution)/shard_map/level/pallas_call | solution.py:32
  12.8 1.6 %collective-permute-start.3 = (f32[68,8,128]{2,1,0:T(8,128)S(1)}, f32[68,8,128]{2,1,0:T(8,128)S(1)}, u32[]{:S(2)}, u32[]{:S(2)}) collective-permute-start(f32[68,8,128]{2,1,0:T(8,128)S(1)} %get-tuple-element.30.held), channel_id=1, source_target_pairs={{0,2},{2,0},{1,3},{3,1},{4,6},{6,4},{5,7},{7,5},{8,10},{10,8},{9,1... | collective-permute-start | bytes 835592 | tf_op jit(solution)/shard_map/ppermute | solution.py:26
  14.4 7.2 %collective-permute-done.3.arrived = f32[68,8,128]{2,1,0:T(8,128)S(1)} collective-permute-done((f32[68,8,128]{2,1,0:T(8,128)S(1)}, f32[68,8,128]{2,1,0:T(8,128)S(1)}, u32[]{:S(2)}, u32[]{:S(2)}) %collective-permute-start.3) | collective-permute-done | bytes 278560 | tf_op jit(solution)/shard_map/ppermute | solution.py:26
  21.7 0.0 copy-start.1
  21.7 0.0 copy-start.2
  21.7 0.0 copy-start.5
  21.7 0.7 %level.3 = (f32[64,8,128]{2,1,0:T(8,128)S(1)}, f32[68,8,128]{2,1,0:T(8,128)S(1)}) custom-call(f32[64,8,128]{2,1,0:T(8,128)S(1)} %get-tuple-element.29.kept, f32[68,8,128]{2,1,0:T(8,128)S(1)} %collective-permute-done.3.arrived, f32[68,8,128]{2,1,0:T(8,128)S(1)} %get-tuple-element.30.held, f32[4,2,16,128]{3,2,1,0:T(8,128)S(1)} %get-tuple-element.25.near, ...), custom_call_target="tpu_custom_call" | custom-call | flops 201326592 | bytes 2277376 | tf_op jit(solution)/shard_map/level/pallas_call | solution.py:32
  22.3 1.6 %collective-permute-start.4 = (f32[68,8,128]{2,1,0:T(8,128)S(1)}, f32[68,8,128]{2,1,0:T(8,128)S(1)}, u32[]{:S(2)}, u32[]{:S(2)}) collective-permute-start(f32[68,8,128]{2,1,0:T(8,128)S(1)} %get-tuple-element.32.held), channel_id=1, source_target_pairs={{0,4},{4,0},{1,5},{5,1},{2,6},{6,2},{3,7},{7,3},{8,12},{12,8},{9,1... | collective-permute-start | bytes 835592 | tf_op jit(solution)/shard_map/ppermute | solution.py:26
  24.0 6.3 %collective-permute-done.4.arrived = f32[68,8,128]{2,1,0:T(8,128)S(1)} collective-permute-done((f32[68,8,128]{2,1,0:T(8,128)S(1)}, f32[68,8,128]{2,1,0:T(8,128)S(1)}, u32[]{:S(2)}, u32[]{:S(2)}) %collective-permute-start.4) | collective-permute-done | bytes 278560 | tf_op jit(solution)/shard_map/ppermute | solution.py:26
  30.3 0.0 copy-done.1
  30.3 0.0 copy-done.2
  30.3 0.0 copy-done.5
  30.3 2.0 %inverse.1 = (f32[16,2,2,16,128]{4,3,2,1,0:T(8,128)}, f32[4,8,128]{2,1,0:T(8,128)S(1)}) custom-call(f32[64,8,128]{2,1,0:T(8,128)S(1)} %get-tuple-element.31.kept, f32[68,8,128]{2,1,0:T(8,128)S(1)} %collective-permute-done.4.arrived, f32[68,8,128]{2,1,0:T(8,128)S(1)} %get-tuple-element.32.held, f32[4,2,16,128]{3,2,1,0:T(8,128)S(1)} %get-tuple-element.25.near, ...), custom_call_target="tpu_custom_call" | custom-call | flops 402653184 | bytes 2572288 | tf_op jit(solution)/shard_map/inverse/pallas_call | solution.py:32
  32.3 4.3 %all-to-all-start = ((f32[16,64,128]{2,1,0:T(8,128)}), f32[16,64,128]{2,1,0:T(8,128)S(1)}, u32[]{:S(2)}, u32[]{:S(2)}) async-start(f32[16,64,128]{2,1,0:T(8,128)} %bitcast.1), calls=%async_computation | async-start | bytes 1048576 | tf_op jit(solution)/shard_map/all_to_all | solution.py:463
  36.6 0.1 blend.1
  36.7 14.2 %all-to-all-done = f32[16,64,128]{2,1,0:T(8,128)S(1)} async-done(((f32[16,64,128]{2,1,0:T(8,128)}), f32[16,64,128]{2,1,0:T(8,128)S(1)}, u32[]{:S(2)}, u32[]{:S(2)}) %all-to-all-start) | async-done | bytes 524320 | tf_op jit(solution)/shard_map/all_to_all | solution.py:463
  50.8 1.2 %turn.1 = f32[2,256,256]{2,1,0:T(8,128)} custom-call(f32[16,2,2,16,128]{4,3,2,1,0:T(8,128)S(1)} %bitcast.5, bf16[256,256]{1,0:T(8,128)(2,1)S(1)} %get-tuple-element.35.blend_high, bf16[256,256]{1,0:T(8,128)(2,1)S(1)} %get-tuple-element.36.blend_low), custom_call_target="tpu_custom_call" | custom-call | flops 201326592 | bytes 1310720 | tf_op jit(solution)/shard_map/turn/pallas_call | solution.py:32
  (2 shorter events, 0.0 us)
Async XLA Ops:
  0.0 7.1 %copy-start.6 = (f32[2,32,128]{2,1,0:T(8,128)S(1)}, f32[2,32,128]{2,1,0:T(8,128)}, u32[]{:S(2)}) copy-start(f32[2,32,128]{2,1,0:T(8,128)} %constant.14.clone.twiddle) | copy-start | bytes 98308
  0.0 0.7 %copy-start.7 = (f32[4,1,2,4,16]{4,3,2,1,0:T(4,128)S(1)}, f32[4,1,2,4,16]{4,3,2,1,0:T(4,128)}, u32[]{:S(2)}) copy-start(f32[4,1,2,4,16]{4,3,2,1,0:T(4,128)} %weight.1) | copy-start | bytes 6148
  0.7 0.7 %copy-start.8 = (s32[4,1,2,8]{3,2,1,0:T(2,128)S(1)}, s32[4,1,2,8]{3,2,1,0:T(2,128)}, u32[]{:S(2)}) copy-start(s32[4,1,2,8]{3,2,1,0:T(2,128)} %shift.1) | copy-start | bytes 772
  1.4 0.7 %copy-start.9 = (f32[4,1,2,8]{3,2,1,0:T(2,128)S(1)}, f32[4,1,2,8]{3,2,1,0:T(2,128)}, u32[]{:S(2)}) copy-start(f32[4,1,2,8]{3,2,1,0:T(2,128)} %phase.1) | copy-start | bytes 772
  2.1 0.7 %copy-start.10 = (s32[4,1,2,16]{3,2,1,0:T(2,128)S(1)}, s32[4,1,2,16]{3,2,1,0:T(2,128)}, u32[]{:S(2)}) copy-start(s32[4,1,2,16]{3,2,1,0:T(2,128)} %offset.1) | copy-start | bytes 1540
  3.0 7.6 %collective-permute-start.1 = (f32[48,128]{1,0:T(8,128)S(1)}, f32[48,128]{1,0:T(8,128)S(1)}, u32[]{:S(2)}, u32[]{:S(2)}) collective-permute-start(f32[48,128]{1,0:T(8,128)S(1)} %get-tuple-element.23.pack), channel_id=1, source_target_pairs={{0,8},{8,0},{1,9},{9,1},{2,10},{10,2},{3,11},{11,3},{4,12},{12,4},... | collective-permute-start | bytes 73736 | tf_op jit(solution)/shard_map/ppermute | solution.py:26
  7.1 1.0 %copy-start = (f32[2,16,4096]{2,1,0:T(8,128)S(1)}, f32[2,16,4096]{2,1,0:T(8,128)}, u32[]{:S(2)}) copy-start(f32[2,16,4096]{2,1,0:T(8,128)} %image.1) | copy-start | bytes 1572868
  8.2 0.9 %copy-start.3 = (bf16[256,256]{1,0:T(8,128)(2,1)S(1)}, bf16[256,256]{1,0:T(8,128)(2,1)}, u32[]{:S(2)}) copy-start(bf16[256,256]{1,0:T(8,128)(2,1)} %constant.13.clone.low_m) | copy-start | bytes 393220
  9.1 0.9 %copy-start.4 = (bf16[256,256]{1,0:T(8,128)(2,1)S(1)}, bf16[256,256]{1,0:T(8,128)(2,1)}, u32[]{:S(2)}) copy-start(bf16[256,256]{1,0:T(8,128)(2,1)} %constant.12.clone.high_m) | copy-start | bytes 393220
  10.5 1.6 %collective-permute-start = (f32[64,8,128]{2,1,0:T(8,128)S(1)}, f32[64,8,128]{2,1,0:T(8,128)S(1)}, u32[]{:S(2)}, u32[]{:S(2)}) collective-permute-start(f32[64,8,128]{2,1,0:T(8,128)S(1)} %get-tuple-element.22), channel_id=1, source_target_pairs={{0,1},{1,0},{2,3},{3,2},{4,5},{5,4},{6,7},{7,6},{8,9},{9,8},{10,11... | collective-permute-start | bytes 786440 | tf_op jit(solution)/shard_map/ppermute | solution.py:26
  10.6 1.5 %collective-permute-start.2 = (f32[32,128]{1,0:T(8,128)S(1)}, f32[32,128]{1,0:T(8,128)S(1)}, u32[]{:S(2)}, u32[]{:S(2)}) collective-permute-start(f32[32,128]{1,0:T(8,128)S(1)} %slice_add_fusion), channel_id=1, source_target_pairs={{0,1},{1,0},{2,3},{3,2},{4,5},{5,4},{6,7},{7,6},{8,9},{9,8},{10,11... | collective-permute-start | bytes 49160 | tf_op jit(solution)/shard_map/ppermute | solution.py:26
  12.8 8.8 %collective-permute-start.3 = (f32[68,8,128]{2,1,0:T(8,128)S(1)}, f32[68,8,128]{2,1,0:T(8,128)S(1)}, u32[]{:S(2)}, u32[]{:S(2)}) collective-permute-start(f32[68,8,128]{2,1,0:T(8,128)S(1)} %get-tuple-element.30.held), channel_id=1, source_target_pairs={{0,2},{2,0},{1,3},{3,1},{4,6},{6,4},{5,7},{7,5},{8,10},{10,8},{9,1... | collective-permute-start | bytes 835592 | tf_op jit(solution)/shard_map/ppermute | solution.py:26
  21.7 8.6 %copy-start.1 = (bf16[256,256]{1,0:T(8,128)(2,1)S(1)}, bf16[256,256]{1,0:T(8,128)(2,1)}, u32[]{:S(2)}) copy-start(bf16[256,256]{1,0:T(8,128)(2,1)} %constant.16.clone.low_m) | copy-start | bytes 393220
  21.7 8.6 %copy-start.2 = (bf16[256,256]{1,0:T(8,128)(2,1)S(1)}, bf16[256,256]{1,0:T(8,128)(2,1)}, u32[]{:S(2)}) copy-start(bf16[256,256]{1,0:T(8,128)(2,1)} %constant.15.clone.high_m) | copy-start | bytes 393220
  21.7 8.6 %copy-start.5 = (f32[2,32,128]{2,1,0:T(8,128)S(1)}, f32[2,32,128]{2,1,0:T(8,128)}, u32[]{:S(2)}) copy-start(f32[2,32,128]{2,1,0:T(8,128)} %constant.17.clone.twiddle) | copy-start | bytes 98308
  22.3 8.0 %collective-permute-start.4 = (f32[68,8,128]{2,1,0:T(8,128)S(1)}, f32[68,8,128]{2,1,0:T(8,128)S(1)}, u32[]{:S(2)}, u32[]{:S(2)}) collective-permute-start(f32[68,8,128]{2,1,0:T(8,128)S(1)} %get-tuple-element.32.held), channel_id=1, source_target_pairs={{0,4},{4,0},{1,5},{5,1},{2,6},{6,2},{3,7},{7,3},{8,12},{12,8},{9,1... | collective-permute-start | bytes 835592 | tf_op jit(solution)/shard_map/ppermute | solution.py:26
  32.3 18.6 %all-to-all-start = ((f32[16,64,128]{2,1,0:T(8,128)}), f32[16,64,128]{2,1,0:T(8,128)S(1)}, u32[]{:S(2)}, u32[]{:S(2)}) async-start(f32[16,64,128]{2,1,0:T(8,128)} %bitcast.1), calls=%async_computation | async-start | bytes 1048576 | tf_op jit(solution)/shard_map/all_to_all | solution.py:463
